TPU v7x, 256 devices: a whole 4x4x8 slice. The times are simulated.
256 devices in a mesh: ctx: 64 (over y, z, core), head: 4 (over x).
Axes of the slice: x: 4, y: 4, z: 8, core: 2. Of those that a mesh axis runs over, the one named last changes fastest.
Arguments:
- query: bfloat16 [64, 2, 512, 4096], P('ctx', None, None, 'head'), may hold values from -48 to 48
- key: bfloat16 [64, 2, 512, 512], P('ctx', None, 'head'), may hold values from -18 to 18
- value: bfloat16 [64, 2, 512, 512], P('ctx', None, 'head'), may hold values from -6 to 6
- d_out: bfloat16 [64, 2, 512, 4096], P('ctx', None, None, 'head'), may hold values from -6 to 6
- doc_start: int32 [512], replicated, may hold values from 0 to 1, as said below
Outputs:
- d_query: bfloat16 [64, 2, 512, 4096], P('ctx', None, None, 'head')
- d_key: bfloat16 [64, 2, 512, 512], P('ctx', None, 'head')
- d_value: bfloat16 [64, 2, 512, 512], P('ctx', None, 'head')
Inputs may be any that keep to these rules, and one draw needn't show every extreme that they name: `doc_start`: 1 where a document begins at that block of 128 tokens (blocks in sequence order); block 0 begins one; from every beginning the next beginning, or the end of the sequence, is 1 to 3 blocks away; the first block of every span after the first lies inside a document of exactly 3 blocks that began in the span before.
All inputs are finite; a program needn't handle non-finite values.
Results may differ from a plain program's by a relative error of at most 0.039.
Values may be sent and summed in bfloat16 or wider, within the bound.
A program may use at most 64 MiB of HBM per device.

v0:
```python
import jax
import jax.numpy as jnp
from jax import lax
from jax.sharding import PartitionSpec as P

HD = 128
BLK = 128
GROUP = 8


def padded_2(cells, sides, width):
    for axis, dim in sides:
        count = lax.axis_size(axis)
        ends = count - 1
        head = lax.slice_in_dim(cells, 0, width, axis=dim)
        tail = lax.slice_in_dim(cells, cells.shape[dim] - width, cells.shape[dim], axis=dim)
        cells = jnp.concatenate(
            [
                lax.ppermute(tail, axis, [(i, (i + 1) % count) for i in range(ends)]),
                cells,
                lax.ppermute(head, axis, [((i + 1) % count, i) for i in range(ends)]),
            ],
            axis=dim,
        )
    return cells


def windowed(extended, reach_rows, blocks):
    pieces = []
    for offset in range(reach_rows // BLK + 1):
        sliced = lax.slice_in_dim(extended, offset * BLK, offset * BLK + blocks * BLK, axis=0)
        pieces.append(sliced.reshape((blocks, BLK) + extended.shape[1:]))
    return jnp.concatenate(pieces, axis=1)


def unwindowed(windows, reach_rows, blocks):
    summed = None
    for offset in range(reach_rows // BLK + 1):
        sliced = windows[:, offset * BLK : (offset + 1) * BLK].reshape(
            (blocks * BLK,) + windows.shape[2:]
        )
        padded = jnp.pad(
            sliced, ((offset * BLK, reach_rows - offset * BLK),) + ((0, 0),) * (windows.ndim - 2)
        )
        summed = padded if summed is None else summed + padded
    return summed


def span_grads(queries, grads_out, keys_ext, values_ext, doc_begins, span_start, reach_rows):
    blocks = queries.shape[0] // BLK
    kv_heads = keys_ext.shape[1] // HD
    score_scale = HD ** (-0.5)
    q_blocks = queries.reshape(blocks, BLK, kv_heads, GROUP, HD)
    do_blocks = grads_out.reshape(blocks, BLK, kv_heads, GROUP, HD)
    k_windows = windowed(keys_ext.reshape(-1, kv_heads, HD), reach_rows, blocks)
    v_windows = windowed(values_ext.reshape(-1, kv_heads, HD), reach_rows, blocks)
    row_pos = jnp.arange(BLK, dtype=jnp.int32)[None, :, None]
    col_pos = jnp.arange(reach_rows + BLK, dtype=jnp.int32)[None, None, :]
    key_pos = (
        span_start - reach_rows + jnp.arange(blocks, dtype=jnp.int32)[:, None, None] * BLK + col_pos
    )
    visible = (col_pos <= row_pos + reach_rows) & (key_pos >= doc_begins[:, None, None])
    visible = visible[:, None, None]
    scores = (
        jnp.einsum("btgjd,bkgd->bgjtk", q_blocks, k_windows, preferred_element_type=jnp.float32)
        * score_scale
    )
    peak = jnp.max(jnp.where(visible, scores, -1e30), axis=-1, keepdims=True)
    weights = jnp.exp(jnp.where(visible, scores - peak, -1e30))
    probs = weights / jnp.sum(weights, axis=-1, keepdims=True)
    probs_b = probs.astype(jnp.bfloat16)
    outputs = jnp.einsum(
        "bgjtk,bkgd->btgjd", probs_b, v_windows, preferred_element_type=jnp.float32
    ).astype(jnp.bfloat16)
    deltas = jnp.sum(do_blocks.astype(jnp.float32) * outputs.astype(jnp.float32), axis=-1)
    dprobs = jnp.einsum(
        "btgjd,bkgd->bgjtk", do_blocks, v_windows, preferred_element_type=jnp.float32
    )
    dscores = (
        probs * (dprobs - jnp.transpose(deltas, (0, 2, 3, 1))[..., None]) * score_scale
    ).astype(jnp.bfloat16)
    d_queries = jnp.einsum(
        "bgjtk,bkgd->btgjd", dscores, k_windows, preferred_element_type=jnp.float32
    ).astype(jnp.bfloat16)
    dk_windows = jnp.einsum(
        "bgjtk,btgjd->bkgd", dscores, q_blocks, preferred_element_type=jnp.float32
    )
    dv_windows = jnp.einsum(
        "bgjtk,btgjd->bkgd", probs_b, do_blocks, preferred_element_type=jnp.float32
    )
    return (
        d_queries.reshape(blocks * BLK, -1),
        unwindowed(dk_windows, reach_rows, blocks).reshape(-1, kv_heads * HD),
        unwindowed(dv_windows, reach_rows, blocks).reshape(-1, kv_heads * HD),
    )


def per_device(query, key, value, d_out, doc_start):
    kv_key, kv_value = (
        lax.all_to_all(key, "head", split_axis=3, concat_axis=2, tiled=True),
        lax.all_to_all(value, "head", split_axis=3, concat_axis=2, tiled=True),
    )
    span_rows = kv_key.shape[2]
    ctx_index = lax.axis_index("ctx")
    ctx_count = lax.axis_size("ctx")
    is_last = ctx_index == ctx_count - 1
    rim_from = span_rows - span_rows
    outgoing = jnp.stack(
        [
            jnp.stack([kv_key[0, 1, rim_from:], kv_value[0, 1, rim_from:]]),
            jnp.stack([kv_key[0, 0, rim_from:], kv_value[0, 0, rim_from:]]),
        ]
    )
    incoming = padded_2(outgoing, (("ctx", 0),), 1)
    previous = [incoming[0], jnp.where(is_last, outgoing[1], incoming[3])]
    run_begin = (
        lax.cummax(
            jnp.where(doc_start == 1, jnp.arange(doc_start.shape[0], dtype=jnp.int32), 0), axis=0
        )
        * BLK
    )
    blocks = span_rows // BLK
    span_results = []
    for span_slot in range(2):
        span_id = ctx_index if span_slot == 0 else 2 * ctx_count - 1 - ctx_index
        span_start = span_id * span_rows
        doc_begins = lax.dynamic_slice_in_dim(run_begin, span_id * blocks, blocks)
        keys_ext = jnp.concatenate([previous[span_slot][0], kv_key[0, span_slot]], axis=0)
        values_ext = jnp.concatenate([previous[span_slot][1], kv_value[0, span_slot]], axis=0)
        span_results.append(
            span_grads(
                query[0, span_slot],
                d_out[0, span_slot],
                keys_ext,
                values_ext,
                doc_begins,
                span_start,
                span_rows,
            )
        )
    partials = jnp.stack(
        [
            jnp.stack([span_results[0][1][:span_rows], span_results[0][2][:span_rows]]),
            jnp.stack([span_results[1][1][:span_rows], span_results[1][2][:span_rows]]),
        ]
    )
    returned = padded_2(partials.astype(jnp.bfloat16), (("ctx", 0),), 1).astype(partials.dtype)
    added_parts = [returned[3] + jnp.where(is_last, partials[1], 0.0), returned[0]]
    key_grads = []
    value_grads = []
    for span_slot in range(2):
        own_key = (
            span_results[span_slot][1][span_rows:].at[rim_from:].add(added_parts[span_slot][0])
        )
        own_value = (
            span_results[span_slot][2][span_rows:].at[rim_from:].add(added_parts[span_slot][1])
        )
        key_grads.append(own_key.astype(jnp.bfloat16))
        value_grads.append(own_value.astype(jnp.bfloat16))
    d_query = jnp.stack([span_results[0][0], span_results[1][0]])[None]
    key_layout = jnp.stack(key_grads)[None]
    value_layout = jnp.stack(value_grads)[None]
    d_key, d_value = (
        lax.all_to_all(key_layout, "head", split_axis=2, concat_axis=3, tiled=True),
        lax.all_to_all(value_layout, "head", split_axis=2, concat_axis=3, tiled=True),
    )
    return (d_query, d_key, d_value)


def solution(mesh):
    return jax.shard_map(
        per_device,
        mesh=mesh,
        in_specs=(
            P("ctx", None, None, "head"),
            P("ctx", None, "head", None),
            P("ctx", None, "head", None),
            P("ctx", None, None, "head"),
            P(),
        ),
        out_specs=(
            P("ctx", None, None, "head"),
            P("ctx", None, "head", None),
            P("ctx", None, "head", None),
        ),
        check_vma=False,
    )
```

profile of v0, /device:TPU:22, one launch (start us, length us, event | category | flops | bytes accessed | tf_op | source)
XLA Modules:
  0.0 142.7 jit_solution(6247647339542804097)
XLA Ops:
  0.6 1.8 %copy.44 = bf16[1,2,128,512]{2,1,0,3:T(2,128)(2,1)} copy(bf16[1,2,128,512]{3,2,1,0:T(8,128)(2,1)} %param.22) | data formatting | bytes 524288 | tf_op args[1]
  2.5 4.8 %all-to-all-start = ((bf16[1,2,128,512]{2,1,0,3:T(2,128)(2,1)}), bf16[1,2,128,512]{2,1,0,3:T(2,128)(2,1)S(1)}, u32[]{:S(2)}, u32[]{:S(2)}) async-start(bf16[1,2,128,512]{2,1,0,3:T(2,128)(2,1)} %copy.44), calls=%async_computation | async-start | bytes 524288 | tf_op jit(solution)/shard_map/all_to_all | solution.py:100
  8.5 1.8 %copy.46 = bf16[1,2,128,512]{2,1,0,3:T(2,128)(2,1)} copy(bf16[1,2,128,512]{3,2,1,0:T(8,128)(2,1)} %param.23) | data formatting | bytes 524288 | tf_op args[2]
  10.4 1.7 %slice_bitcast_fusion.1 = (bf16[64,8,8,128]{3,1,2,0:T(8,128)(2,1)S(1)}, bf16[64,8,8,128]{3,1,2,0:T(8,128)(2,1)S(1)}) fusion(bf16[1,2,512,1024]{3,2,1,0:T(8,128)(2,1)} %param.21), kind=kLoop, calls=%fused_computation.56 | loop fusion | bytes 4194304
  12.1 4.6 %slice_bitcast_fusion.3 = (bf16[64,8,8,128]{3,1,2,0:T(8,128)(2,1)}, f32[64,8,8,128]{3,1,2,0:T(8,128)}, f32[64,8,8,128]{3,1,2,0:T(8,128)}, bf16[64,8,8,128]{3,1,2,0:T(8,128)(2,1)}) fusion(bf16[1,2,512,1024]{3,2,1,0:T(8,128)(2,1)} %param.24), kind=kLoop, calls=%fused_computation.68 | loop fusion | flops 1048576 | bytes 8388608
  16.8 4.8 %all-to-all-start.1 = ((bf16[1,2,128,512]{2,1,0,3:T(2,128)(2,1)}), bf16[1,2,128,512]{2,1,0,3:T(2,128)(2,1)S(1)}, u32[]{:S(2)}, u32[]{:S(2)}) async-start(bf16[1,2,128,512]{2,1,0,3:T(2,128)(2,1)} %copy.46), calls=%async_computation.1 | async-start | bytes 524288 | tf_op jit(solution)/shard_map/all_to_all | solution.py:101
  22.5 3.7 %all-to-all-done.1 = bf16[1,2,128,512]{2,1,0,3:T(2,128)(2,1)S(1)} async-done(((bf16[1,2,128,512]{2,1,0,3:T(2,128)(2,1)}), bf16[1,2,128,512]{2,1,0,3:T(2,128)(2,1)S(1)}, u32[]{:S(2)}, u32[]{:S(2)}) %all-to-all-start.1) | async-done | bytes 262176 | tf_op jit(solution)/shard_map/all_to_all | solution.py:101
  26.4 1.0 fusion.102
  28.1 5.2 %collective-permute-start.1 = (bf16[1,2,512,128]{3,2,1,0:T(8,128)(2,1)}, bf16[1,2,512,128]{3,2,1,0:T(8,128)(2,1)}, u32[]{:S(2)}, u32[]{:S(2)}) collective-permute-start(bf16[1,2,512,128]{3,2,1,0:T(8,128)(2,1)} %maximum_bitcast_fusion.1), channel_id=1, source_target_pairs={{4,0},{8,4},{12,8},{16,12},{20,16},{24,20},{28,24},{32,28},{36,32}... | collective-permute-start | bytes 786440 | tf_op jit(solution)/shard_map/ppermute | solution.py:21
  34.0 2.5 %copy.98 = bf16[64,8,8,128]{3,2,1,0:T(8,128)(2,1)} copy(bf16[64,8,8,128]{3,1,2,0:T(8,128)(2,1)} %get-tuple-element.83) | data formatting | bytes 2097152
  36.4 1.5 %copy.101 = bf16[64,8,8,128]{3,2,1,0:T(8,128)(2,1)S(1)} copy(bf16[64,8,8,128]{3,1,2,0:T(8,128)(2,1)} %get-tuple-element.86) | data formatting | bytes 2097152
  37.9 3.4 %copy.99 = f32[64,8,8,128]{3,2,1,0:T(8,128)} copy(f32[64,8,8,128]{3,1,2,0:T(8,128)} %get-tuple-element.84) | data formatting | bytes 4194304
  41.4 2.9 %copy.52 = f32[4,128,1,8,128]{1,4,3,0,2:T(8,128)} copy(f32[4,128,1,8,128]{4,3,2,1,0:T(8,128)} %bitcast.414) | data formatting | bytes 4194304 | tf_op jit(solution)/shard_map/convert_element_type | solution.py:75
  44.2 3.4 %copy.102 = f32[64,8,8,128]{3,2,1,0:T(8,128)} copy(f32[64,8,8,128]{3,1,2,0:T(8,128)} %get-tuple-element.85) | data formatting | bytes 4194304
  47.6 2.9 %copy.60 = f32[4,128,1,8,128]{1,4,3,0,2:T(8,128)} copy(f32[4,128,1,8,128]{4,3,2,1,0:T(8,128)} %bitcast.415) | data formatting | bytes 4194304 | tf_op jit(solution)/shard_map/convert_element_type | solution.py:75
  50.5 2.2 %broadcast_and_fusion.1 = (pred[4,128,640]{1,2,0:T(8,128)(4,1)S(1)}, pred[4,128,640]{1,2,0:T(8,128)(4,1)S(1)}) fusion(pred[4,640]{1,0:T(4,128)(4,1)S(1)} %get-tuple-element.162, pred[128,640]{0,1:T(8,128)(4,1)} %iota_compare_fusion, pred[4,640]{1,0:T(4,128)(4,1)S(1)} %get-tuple-element.161), kind=kLoop, calls=%fused_computation.78 | loop fusion | flops 655360 | bytes 742400 | tf_op jit(solution)/shard_map/and | solution.py:62
  52.7 1.8 %fusion.81 = (bf16[1,2,512,128]{3,2,1,0:T(8,128)(2,1)}, bf16[2,512,128]{2,1,0:T(8,128)(2,1)S(1)}) fusion(bf16[1,512,128]{2,1,0:T(8,128)(2,1)} %get-tuple-element.159, bf16[1,512,128]{2,1,0:T(8,128)(2,1)} %get-tuple-element.114, bf16[1,2,512,128]{3,2,1,0:T(8,128)(2,1)} %collective-permute-done.1, pred[]{:T(512)S(6)} %eq.11), kind=kLoop, calls=%fused_computation.125 | loop fusion | flops 262144 | bytes 1048577 | tf_op jit(solution)/shard_map/stack | solution.py:108
  54.6 2.1 %collective-permute-start = (bf16[1,2,512,128]{3,2,1,0:T(8,128)(2,1)}, bf16[1,2,512,128]{3,2,1,0:T(8,128)(2,1)}, u32[]{:S(2)}, u32[]{:S(2)}) collective-permute-start(bf16[1,2,512,128]{3,2,1,0:T(8,128)(2,1)} %get-tuple-element.135), channel_id=1, source_target_pairs={{0,4},{4,8},{8,12},{12,16},{16,20},{20,24},{24,28},{28,32},{32,36}... | collective-permute-start | bytes 786440 | tf_op jit(solution)/shard_map/ppermute | solution.py:19
  58.0 1.6 %fusion.6 = (f32[4,8,128]{2,1,0:T(8,128)S(1)}, f32[4,640,128,8]{2,1,3,0:T(8,128)S(1)}) fusion(pred[4,128,640]{1,2,0:T(8,128)(4,1)S(1)} %get-tuple-element.148, bf16[4,128,8,128]{3,2,1,0:T(8,128)(2,1)S(1)} %bitcast.412, bf16[4,640,1,128]{3,1,0,2:T(8,128)(2,1)S(1)} %constant_dynamic-update-slice_fusion.10), kind=kOutput, calls=%fused_computation.10 | convolution fusion | flops 678948864 | bytes 12533760 | tf_op jit(solution)/shard_map/btgjd,bkgd->bgjtk/dot_general | solution.py:65
  59.7 2.4 %fusion.15 = f32[4,8,128]{2,1,0:T(8,128)S(1)} fusion(f32[4,640,128,8]{2,1,3,0:T(8,128)S(1)} %get-tuple-element.152, f32[4,8,128]{2,1,0:T(8,128)S(1)} %get-tuple-element.151, pred[4,128,640]{1,2,0:T(8,128)(4,1)S(1)} %get-tuple-element.148), kind=kLoop, calls=%fused_computation.21 | loop fusion | flops 10481664 | bytes 10846208 | tf_op jit(solution)/shard_map/reduce_sum | solution.py:70
  62.1 3.1 %fusion.41 = f32[4,640,1,128]{3,1,0,2:T(8,128)S(1)} fusion(bf16[4,128,8,128]{3,2,1,0:T(8,128)(2,1)S(1)} %bitcast.439, f32[4,8,128]{2,1,0:T(8,128)S(1)} %fusion.15, f32[4,8,128]{2,1,0:T(8,128)S(1)} %get-tuple-element.151, f32[4,640,128,8]{2,1,3,0:T(8,128)S(1)} %get-tuple-element.152, pred[4,128,640]{1,2,0:T(8,128)(4,1)S(1)} %get-tuple-element.148), kind=kOutput, calls=%fused_computation.50 | convolution fusion | flops 684195840 | bytes 13205504 | tf_op jit(solution)/shard_map/bgjtk,btgjd->bkgd/dot_general | solution.py:88
  65.2 3.2 %fusion.29 = f32[4,128,8]{1,2,0:T(8,128)S(1)} fusion(f32[4,128,1,8,128]{1,4,3,0,2:T(8,128)S(1)} %copy-done.6, bf16[4,640,1,128]{3,1,0,2:T(8,128)(2,1)S(1)} %constant_dynamic-update-slice_fusion.15, f32[4,8,128]{2,1,0:T(8,128)S(1)} %fusion.15, f32[4,8,128]{2,1,0:T(8,128)S(1)} %get-tuple-element.151, f32[4,640,128,8]{2,1,3,0:T(8,128)S(1)} %get-tuple-element.152, ...), kind=kOutput, calls=%fused_computation.37 | convolution fusion | flops 686288896 | bytes 13615104 | tf_op jit(solution)/shard_map/bgjtk,bkgd->btgjd/dot_general | solution.py:72
  68.4 4.2 %fusion.17 = bf16[4,8,128,640]{2,3,1,0:T(8,128)(2,1)S(1)} fusion(f32[4,8,128]{2,1,0:T(8,128)S(1)} %bitcast.468, f32[4,8,128]{2,1,0:T(8,128)S(1)} %fusion.15, f32[4,8,128]{2,1,0:T(8,128)S(1)} %get-tuple-element.151, f32[4,640,128,8]{2,1,3,0:T(8,128)S(1)} %get-tuple-element.152, pred[4,128,640]{1,2,0:T(8,128)(4,1)S(1)} %get-tuple-element.148, ...), kind=kOutput, calls=%fused_computation.23 | convolution fusion | flops 692060160 | bytes 17809408 | tf_op jit(solution)/shard_map/btgjd,bkgd->bgjtk/dot_general | solution.py:76
  72.8 1.5 %convolution_bitcast_fusion = f32[4,640,1,128]{3,1,0,2:T(8,128)S(1)} fusion(bf16[4,8,128,640]{2,3,1,0:T(8,128)(2,1)S(1)} %fusion.17, bf16[4,128,8,128]{3,2,1,0:T(8,128)(2,1)S(1)} %bitcast.413), kind=kOutput, calls=%fused_computation.47 | convolution fusion | flops 671088640 | bytes 7602176 | tf_op jit(solution)/shard_map/bgjtk,btgjd->bkgd/dot_general | solution.py:85
  75.4 2.1 %collective-permute-start.2 = (bf16[1,2,512,128]{3,2,1,0:T(8,128)(2,1)S(1)}, bf16[1,2,512,128]{3,2,1,0:T(8,128)(2,1)S(1)}, u32[]{:S(2)}, u32[]{:S(2)}) collective-permute-start(bf16[1,2,512,128]{3,2,1,0:T(8,128)(2,1)S(1)} %fusion.76), channel_id=1, source_target_pairs={{0,4},{4,8},{8,12},{12,16},{16,20},{20,24},{24,28},{28,32},{32,36}... | collective-permute-start | bytes 786440 | tf_op jit(solution)/shard_map/ppermute | solution.py:19
  77.5 1.0 slice_bitcast_fusion.12
  79.0 1.6 %fusion.9 = (f32[4,8,128]{2,1,0:T(8,128)S(1)}, f32[4,640,128,8]{2,1,3,0:T(8,128)S(1)}) fusion(pred[4,128,640]{1,2,0:T(8,128)(4,1)S(1)} %get-tuple-element.147, bf16[4,128,8,128]{3,2,1,0:T(8,128)(2,1)S(1)} %bitcast.410, bf16[4,640,1,128]{3,1,0,2:T(8,128)(2,1)S(1)} %constant_dynamic-update-slice_fusion), kind=kOutput, calls=%fused_computation.15 | convolution fusion | flops 678948864 | bytes 12533760 | tf_op jit(solution)/shard_map/btgjd,bkgd->bgjtk/dot_general | solution.py:65
  80.7 2.4 %fusion.13 = f32[4,8,128]{2,1,0:T(8,128)S(1)} fusion(f32[4,640,128,8]{2,1,3,0:T(8,128)S(1)} %get-tuple-element.154, f32[4,8,128]{2,1,0:T(8,128)S(1)} %get-tuple-element.153, pred[4,128,640]{1,2,0:T(8,128)(4,1)S(1)} %get-tuple-element.147), kind=kLoop, calls=%fused_computation.19 | loop fusion | flops 10481664 | bytes 10846208 | tf_op jit(solution)/shard_map/reduce_sum | solution.py:70
  83.1 4.2 %fusion.38 = f32[4,640,1,128]{3,1,0,2:T(8,128)S(1)} fusion(bf16[4,128,8,128]{3,2,1,0:T(8,128)(2,1)} %bitcast.437, f32[4,8,128]{2,1,0:T(8,128)S(1)} %fusion.13, f32[4,8,128]{2,1,0:T(8,128)S(1)} %get-tuple-element.153, f32[4,640,128,8]{2,1,3,0:T(8,128)S(1)} %get-tuple-element.154, pred[4,128,640]{1,2,0:T(8,128)(4,1)S(1)} %get-tuple-element.147), kind=kOutput, calls=%fused_computation.49 | convolution fusion | flops 684195840 | bytes 13205504 | tf_op jit(solution)/shard_map/bgjtk,btgjd->bkgd/dot_general | solution.py:88
  87.3 4.4 %fusion.31 = f32[4,128,8]{1,2,0:T(8,128)S(1)} fusion(f32[4,128,1,8,128]{1,4,3,0,2:T(8,128)S(1)} %copy-done.5, bf16[4,640,1,128]{3,1,0,2:T(8,128)(2,1)} %copy-done.14, f32[4,8,128]{2,1,0:T(8,128)S(1)} %fusion.13, f32[4,8,128]{2,1,0:T(8,128)S(1)} %get-tuple-element.153, f32[4,640,128,8]{2,1,3,0:T(8,128)S(1)} %get-tuple-element.154, ...), kind=kOutput, calls=%fused_computation.40 | convolution fusion | flops 686288896 | bytes 13615104 | tf_op jit(solution)/shard_map/bgjtk,bkgd->btgjd/dot_general | solution.py:72
  91.7 4.2 %fusion.16 = bf16[4,8,128,640]{2,3,1,0:T(8,128)(2,1)S(1)} fusion(f32[4,8,128]{2,1,0:T(8,128)S(1)} %bitcast.469, f32[4,8,128]{2,1,0:T(8,128)S(1)} %fusion.13, f32[4,8,128]{2,1,0:T(8,128)S(1)} %get-tuple-element.153, f32[4,640,128,8]{2,1,3,0:T(8,128)S(1)} %get-tuple-element.154, pred[4,128,640]{1,2,0:T(8,128)(4,1)S(1)} %get-tuple-element.147, ...), kind=kOutput, calls=%fused_computation.22 | convolution fusion | flops 692060160 | bytes 17809408 | tf_op jit(solution)/shard_map/btgjd,bkgd->bgjtk/dot_general | solution.py:76
  96.2 2.1 %copy-done = bf16[4,8,128,640]{2,3,1,0:T(8,128)(2,1)} copy-done((bf16[4,8,128,640]{2,3,1,0:T(8,128)(2,1)}, bf16[4,8,128,640]{2,3,1,0:T(8,128)(2,1)S(1)}, u32[]{:S(2)}) %copy-start) | copy-done | bytes 5242904
  98.3 1.5 %convolution_bitcast_fusion.1 = f32[4,640,1,128]{3,1,0,2:T(8,128)S(1)} fusion(bf16[4,8,128,640]{2,3,1,0:T(8,128)(2,1)S(1)} %fusion.16, bf16[4,128,8,128]{3,2,1,0:T(8,128)(2,1)S(1)} %bitcast.411), kind=kOutput, calls=%fused_computation.48 | convolution fusion | flops 671088640 | bytes 7602176 | tf_op jit(solution)/shard_map/bgjtk,btgjd->bkgd/dot_general | solution.py:85
  100.8 6.0 %collective-permute-start.3 = (bf16[1,2,512,128]{3,2,1,0:T(8,128)(2,1)S(1)}, bf16[1,2,512,128]{3,2,1,0:T(8,128)(2,1)S(1)}, u32[]{:S(2)}, u32[]{:S(2)}) collective-permute-start(bf16[1,2,512,128]{3,2,1,0:T(8,128)(2,1)S(1)} %maximum_bitcast_fusion.2), channel_id=1, source_target_pairs={{4,0},{8,4},{12,8},{16,12},{20,16},{24,20},{28,24},{32,28},{36,32}... | collective-permute-start | bytes 786440 | tf_op jit(solution)/shard_map/ppermute | solution.py:21
  106.9 2.0 %fusion.45 = bf16[4,128,1,8,128]{1,4,3,0,2:T(8,128)(2,1)} fusion(bf16[4,8,128,640]{2,3,1,0:T(8,128)(2,1)S(1)} %fusion.17, bf16[4,640,1,128]{3,1,0,2:T(8,128)(2,1)S(1)} %constant_dynamic-update-slice_fusion.10), kind=kOutput, calls=%fused_computation.52 | convolution fusion | flops 671612928 | bytes 6946816 | tf_op jit(solution)/shard_map/bgjtk,bkgd->btgjd/dot_general | solution.py:82
  108.9 1.7 %copy.63 = bf16[4,128,1,8,128]{4,3,1,0,2:T(8,128)(2,1)S(1)} copy(bf16[4,128,1,8,128]{1,4,3,0,2:T(8,128)(2,1)} %fusion.45) | data formatting | bytes 2097152 | tf_op jit(solution)/shard_map/convert_element_type | solution.py:84
  110.6 1.3 stack_reshape.7
  111.9 1.2 fusion.79
  113.1 1.0 fusion.78
  115.1 5.3 %all-to-all-start.3 = ((bf16[1,2,512,128]{3,1,0,2:T(2,128)(2,1)}), bf16[1,2,512,128]{3,1,0,2:T(2,128)(2,1)S(1)}, u32[]{:S(2)}, u32[]{:S(2)}) async-start(bf16[1,2,512,128]{3,1,0,2:T(2,128)(2,1)} %copy.71), calls=%async_computation.3 | async-start | bytes 524288 | tf_op jit(solution)/shard_map/all_to_all | solution.py:165
  120.5 1.2 add_convert_fusion
  121.9 1.3 maximum_bitcast_fusion.3
  123.2 1.8 %all-to-all-done.3 = bf16[1,2,512,128]{3,1,0,2:T(2,128)(2,1)S(1)} async-done(((bf16[1,2,512,128]{3,1,0,2:T(2,128)(2,1)}), bf16[1,2,512,128]{3,1,0,2:T(2,128)(2,1)S(1)}, u32[]{:S(2)}, u32[]{:S(2)}) %all-to-all-start.3) | async-done | bytes 262176 | tf_op jit(solution)/shard_map/all_to_all | solution.py:165
  125.0 5.4 %all-to-all-start.2 = ((bf16[1,2,512,128]{3,1,0,2:T(2,128)(2,1)}), bf16[1,2,512,128]{3,1,0,2:T(2,128)(2,1)S(1)}, u32[]{:S(2)}, u32[]{:S(2)}) async-start(bf16[1,2,512,128]{3,1,0,2:T(2,128)(2,1)} %maximum_bitcast_fusion.3), calls=%async_computation.2 | async-start | bytes 524288 | tf_op jit(solution)/shard_map/all_to_all | solution.py:164
  130.5 4.5 %fusion.44 = bf16[4,128,1,8,128]{1,4,3,0,2:T(8,128)(2,1)} fusion(bf16[4,8,128,640]{2,3,1,0:T(8,128)(2,1)} %copy-done, bf16[4,640,1,128]{3,1,0,2:T(8,128)(2,1)S(1)} %constant_dynamic-update-slice_fusion), kind=kOutput, calls=%fused_computation.51 | convolution fusion | flops 671612928 | bytes 6946816 | tf_op jit(solution)/shard_map/bgjtk,bkgd->btgjd/dot_general | solution.py:82
  135.0 1.7 %copy.55 = bf16[4,128,1,8,128]{4,3,1,0,2:T(8,128)(2,1)S(1)} copy(bf16[4,128,1,8,128]{1,4,3,0,2:T(8,128)(2,1)} %fusion.44) | data formatting | bytes 2097152 | tf_op jit(solution)/shard_map/convert_element_type | solution.py:84
  136.7 1.3 stack_reshape.6
  138.0 2.7 %maximum_bitcast_fusion = bf16[1,2,512,1024]{3,2,1,0:T(8,128)(2,1)} fusion(bf16[1,512,1024]{2,1,0:T(8,128)(2,1)S(1)} %copy-done.1, bf16[1,512,1024]{2,1,0:T(8,128)(2,1)} %stack_reshape.6), kind=kLoop, calls=%fused_computation.34 | loop fusion | flops 1048576 | bytes 4194304 | tf_op jit(solution)/shard_map/broadcast_in_dim | solution.py:160
  (102 shorter events, 11.1 us)
Async XLA Ops:
  2.5 14.3 %all-to-all-start = ((bf16[1,2,128,512]{2,1,0,3:T(2,128)(2,1)}), bf16[1,2,128,512]{2,1,0,3:T(2,128)(2,1)S(1)}, u32[]{:S(2)}, u32[]{:S(2)}) async-start(bf16[1,2,128,512]{2,1,0,3:T(2,128)(2,1)} %copy.44), calls=%async_computation | async-start | bytes 524288 | tf_op jit(solution)/shard_map/all_to_all | solution.py:100
  16.8 9.4 %all-to-all-start.1 = ((bf16[1,2,128,512]{2,1,0,3:T(2,128)(2,1)}), bf16[1,2,128,512]{2,1,0,3:T(2,128)(2,1)S(1)}, u32[]{:S(2)}, u32[]{:S(2)}) async-start(bf16[1,2,128,512]{2,1,0,3:T(2,128)(2,1)} %copy.46), calls=%async_computation.1 | async-start | bytes 524288 | tf_op jit(solution)/shard_map/all_to_all | solution.py:101
  28.1 24.6 %collective-permute-start.1 = (bf16[1,2,512,128]{3,2,1,0:T(8,128)(2,1)}, bf16[1,2,512,128]{3,2,1,0:T(8,128)(2,1)}, u32[]{:S(2)}, u32[]{:S(2)}) collective-permute-start(bf16[1,2,512,128]{3,2,1,0:T(8,128)(2,1)} %maximum_bitcast_fusion.1), channel_id=1, source_target_pairs={{4,0},{8,4},{12,8},{16,12},{20,16},{24,20},{28,24},{32,28},{36,32}... | collective-permute-start | bytes 786440 | tf_op jit(solution)/shard_map/ppermute | solution.py:21
  54.6 23.0 %collective-permute-start = (bf16[1,2,512,128]{3,2,1,0:T(8,128)(2,1)}, bf16[1,2,512,128]{3,2,1,0:T(8,128)(2,1)}, u32[]{:S(2)}, u32[]{:S(2)}) collective-permute-start(bf16[1,2,512,128]{3,2,1,0:T(8,128)(2,1)} %get-tuple-element.135), channel_id=1, source_target_pairs={{0,4},{4,8},{8,12},{12,16},{16,20},{20,24},{24,28},{28,32},{32,36}... | collective-permute-start | bytes 786440 | tf_op jit(solution)/shard_map/ppermute | solution.py:19
  62.1 3.1 %copy-start.6 = (f32[4,128,1,8,128]{1,4,3,0,2:T(8,128)S(1)}, f32[4,128,1,8,128]{1,4,3,0,2:T(8,128)}, u32[]{:S(2)}) copy-start(f32[4,128,1,8,128]{1,4,3,0,2:T(8,128)} %copy.60) | copy-start | bytes 6291460
  72.6 6.0 %copy-start.11 = (bf16[512,128]{1,0:T(8,128)(2,1)S(1)}, bf16[512,128]{1,0:T(8,128)(2,1)}, u32[]{:S(2)}) copy-start(bf16[512,128]{1,0:T(8,128)(2,1)} %get-tuple-element.115) | copy-start | bytes 393220
  72.6 6.1 %copy-start.10 = (bf16[512,128]{1,0:T(8,128)(2,1)S(1)}, bf16[512,128]{1,0:T(8,128)(2,1)}, u32[]{:S(2)}) copy-start(bf16[512,128]{1,0:T(8,128)(2,1)} %get-tuple-element.158) | copy-start | bytes 393220
  72.8 6.1 %copy-start.13 = (bf16[1,1,512,128]{3,2,1,0:T(8,128)(2,1)S(1)}, bf16[1,1,512,128]{3,2,1,0:T(8,128)(2,1)}, u32[]{:S(2)}) copy-start(bf16[1,1,512,128]{3,2,1,0:T(8,128)(2,1)} %get-tuple-element.160) | copy-start | bytes 393220
  72.8 6.2 %copy-start.12 = (bf16[1,1,512,128]{3,2,1,0:T(8,128)(2,1)S(1)}, bf16[1,1,512,128]{3,2,1,0:T(8,128)(2,1)}, u32[]{:S(2)}) copy-start(bf16[1,1,512,128]{3,2,1,0:T(8,128)(2,1)} %get-tuple-element.113) | copy-start | bytes 393220
  75.2 5.4 %copy-start.2 = (f32[1,512,128]{2,1,0:T(8,128)}, f32[1,512,128]{2,1,0:T(8,128)S(1)}, u32[]{:S(2)}) copy-start(f32[1,512,128]{2,1,0:T(8,128)S(1)} %get-tuple-element.111) | copy-start | bytes 786436
  75.3 5.4 %copy-start.4 = (f32[1024,1,128]{2,0,1:T(8,128)}, f32[1024,1,128]{2,0,1:T(8,128)S(1)}, u32[]{:S(2)}) copy-start(f32[1024,1,128]{2,0,1:T(8,128)S(1)} %pad_add_fusion.1) | copy-start | bytes 1572868
  75.4 36.5 %collective-permute-start.2 = (bf16[1,2,512,128]{3,2,1,0:T(8,128)(2,1)S(1)}, bf16[1,2,512,128]{3,2,1,0:T(8,128)(2,1)S(1)}, u32[]{:S(2)}, u32[]{:S(2)}) collective-permute-start(bf16[1,2,512,128]{3,2,1,0:T(8,128)(2,1)S(1)} %fusion.76), channel_id=1, source_target_pairs={{0,4},{4,8},{8,12},{12,16},{16,20},{20,24},{24,28},{28,32},{32,36}... | collective-permute-start | bytes 786440 | tf_op jit(solution)/shard_map/ppermute | solution.py:19
  78.9 4.2 %copy-start.14 = (bf16[4,640,1,128]{3,1,0,2:T(8,128)(2,1)}, bf16[4,640,1,128]{3,1,0,2:T(8,128)(2,1)S(1)}, u32[]{:S(2)}) copy-start(bf16[4,640,1,128]{3,1,0,2:T(8,128)(2,1)S(1)} %constant_dynamic-update-slice_fusion.5) | copy-start | bytes 1966084
  83.1 4.2 %copy-start.5 = (f32[4,128,1,8,128]{1,4,3,0,2:T(8,128)S(1)}, f32[4,128,1,8,128]{1,4,3,0,2:T(8,128)}, u32[]{:S(2)}) copy-start(f32[4,128,1,8,128]{1,4,3,0,2:T(8,128)} %copy.52) | copy-start | bytes 6291460
  87.3 4.4 %copy-start.9 = (bf16[64,8,8,128]{3,2,1,0:T(8,128)(2,1)S(1)}, bf16[64,8,8,128]{3,2,1,0:T(8,128)(2,1)}, u32[]{:S(2)}) copy-start(bf16[64,8,8,128]{3,2,1,0:T(8,128)(2,1)} %copy.98) | copy-start | bytes 3145732
  87.3 4.4 %copy-start.15 = (bf16[4,640,1,128]{3,1,0,2:T(8,128)(2,1)S(1)}, bf16[4,640,1,128]{3,1,0,2:T(8,128)(2,1)}, u32[]{:S(2)}) copy-start(bf16[4,640,1,128]{3,1,0,2:T(8,128)(2,1)} %copy-done.14) | copy-start | bytes 1966084
  96.0 2.3 %copy-start = (bf16[4,8,128,640]{2,3,1,0:T(8,128)(2,1)}, bf16[4,8,128,640]{2,3,1,0:T(8,128)(2,1)S(1)}, u32[]{:S(2)}) copy-start(bf16[4,8,128,640]{2,3,1,0:T(8,128)(2,1)S(1)} %fusion.16) | copy-start | bytes 15728644
  96.1 10.7 %copy-start.7 = (f32[1024,1,128]{2,0,1:T(8,128)}, f32[1024,1,128]{2,0,1:T(8,128)S(1)}, u32[]{:S(2)}) copy-start(f32[1024,1,128]{2,0,1:T(8,128)S(1)} %pad_add_fusion) | copy-start | bytes 1572868
  99.8 12.1 %copy-start.3 = (f32[1,512,128]{2,1,0:T(8,128)S(1)}, f32[1,512,128]{2,1,0:T(8,128)}, u32[]{:S(2)}) copy-start(f32[1,512,128]{2,1,0:T(8,128)} %copy-done.2) | copy-start | bytes 786436
  100.0 0.8 copy-start.8
  100.8 11.0 %collective-permute-start.3 = (bf16[1,2,512,128]{3,2,1,0:T(8,128)(2,1)S(1)}, bf16[1,2,512,128]{3,2,1,0:T(8,128)(2,1)S(1)}, u32[]{:S(2)}, u32[]{:S(2)}) collective-permute-start(bf16[1,2,512,128]{3,2,1,0:T(8,128)(2,1)S(1)} %maximum_bitcast_fusion.2), channel_id=1, source_target_pairs={{4,0},{8,4},{12,8},{16,12},{20,16},{24,20},{28,24},{32,28},{36,32}... | collective-permute-start | bytes 786440 | tf_op jit(solution)/shard_map/ppermute | solution.py:21
  111.8 26.1 %copy-start.1 = (bf16[1,512,1024]{2,1,0:T(8,128)(2,1)S(1)}, bf16[1,512,1024]{2,1,0:T(8,128)(2,1)}, u32[]{:S(2)}) copy-start(bf16[1,512,1024]{2,1,0:T(8,128)(2,1)} %stack_reshape.7) | copy-start | bytes 3145732
  115.1 9.9 %all-to-all-start.3 = ((bf16[1,2,512,128]{3,1,0,2:T(2,128)(2,1)}), bf16[1,2,512,128]{3,1,0,2:T(2,128)(2,1)S(1)}, u32[]{:S(2)}, u32[]{:S(2)}) async-start(bf16[1,2,512,128]{3,1,0,2:T(2,128)(2,1)} %copy.71), calls=%async_computation.3 | async-start | bytes 524288 | tf_op jit(solution)/shard_map/all_to_all | solution.py:165
  125.0 16.7 %all-to-all-start.2 = ((bf16[1,2,512,128]{3,1,0,2:T(2,128)(2,1)}), bf16[1,2,512,128]{3,1,0,2:T(2,128)(2,1)S(1)}, u32[]{:S(2)}, u32[]{:S(2)}) async-start(bf16[1,2,512,128]{3,1,0,2:T(2,128)(2,1)} %maximum_bitcast_fusion.3), calls=%async_computation.2 | async-start | bytes 524288 | tf_op jit(solution)/shard_map/all_to_all | solution.py:164
where the time goes:
time: 144 us; the launch traced here: 143 us
  local copies, waits for them, and re-layouts  39.7 us (28%)
  matrix products  36.2 us (25%)
  starting transfers between devices  35.8 us (25%)
  other arithmetic  24.1 us (17%)
  waiting for transfers between devices  5.58 us (4%)
    unnamed x57, local copies, waits for them, and re-layouts  19.9 us
    ppermute x2, starting transfers between devices, padded_2(): lax.ppermute(head, axis, [((i + 1) % count, i) for i in range(ends)])  11.2 us
    dot_general x2, matrix products, span_grads(): jnp.einsum('btgjd,bkgd->bgjtk', do_blocks, v_windows, preferred_element_t...  8.42 us
    dot_general x2, matrix products, span_grads(): jnp.einsum('bgjtk,bkgd->btgjd', probs_b, v_windows, preferred_element_typ...  7.54 us
    dot_general x2, matrix products, span_grads(): jnp.einsum('bgjtk,btgjd->bkgd', probs_b, do_blocks, preferred_element_typ...  7.32 us
    dot_general x2, matrix products, span_grads(): jnp.einsum('bgjtk,bkgd->btgjd', dscores, k_windows, preferred_element_typ...  6.55 us
    convert_element_type x2, local copies, waits for them, and re-layouts, span_grads(): do_blocks.astype(jnp.float32) * outputs.astype(jnp.float32)  5.78 us
    all_to_all x1, starting transfers between devices, per_device(): lax.all_to_all(key_layout, 'head', split_axis=2, concat_axis=3, tiled=True)  5.45 us
  transfers between devices with their start and end apart: 8, of which 2 were waited for; matrix products, arithmetic and copies ran while one was open for 61% of the time, Pallas kernels for 0%

commit v1 on v0

v1 whole, which is shorter than its diff:
```python
import functools

import jax
import jax.numpy as jnp
from jax import lax
from jax.experimental import pallas as pl
from jax.experimental.pallas import tpu as pltpu
from jax.sharding import PartitionSpec as P

F32 = jnp.float32
BF16 = jnp.bfloat16
HD = 128
BLK = 128
HEADS = 8
SPAN = 512
TAIL = 256
EXT = TAIL + SPAN
SCALE = HD**-0.5
SCALE_LOG2E = SCALE * 1.4426950408889634
BIG = 1e30
NT = (((1,), (1,)), ((), ()))
NN = (((1,), (0,)), ((), ()))
MESH = pl.DeviceIdType.MESH


def dot(a, b, dims=NN):
    return lax.dot_general(a, b, dims, preferred_element_type=F32)


def at_block(index):
    if isinstance(index, int):
        return index * BLK
    return pl.multiple_of(index * BLK, BLK)


def block_grads(q_v, do_v, dq_v, kv, acc, docs, tri, slot, span, qb, k0, nk):
    rows = pl.ds(at_block(qb), BLK)
    krows = pl.ds(at_block(k0), nk * BLK)
    kw = kv[0, slot, krows, :]
    vw = kv[1, slot, krows, :]
    g = span * 4 + qb
    hidden = docs[g]
    hide = [hidden]
    for back in range(1, nk - 1):
        hidden = hidden + docs[jnp.maximum(g - back, 0)]
        hide.append(hidden)
    subs = [jnp.where(x > 0, BIG, 0.0).astype(F32) for x in hide][::-1]
    qq = q_v[slot, rows, :]
    dd = do_v[slot, rows, :]
    q2 = jnp.concatenate([qq[:, h * HD : (h + 1) * HD] for h in range(HEADS)], axis=0)
    d2 = jnp.concatenate([dd[:, h * HD : (h + 1) * HD] for h in range(HEADS)], axis=0)
    scores = dot(kw, q2, NT)
    dprobs = dot(vw, d2, NT)
    parts = [scores[i * BLK : (i + 1) * BLK] for i in range(nk)]
    parts[-1] = parts[-1] + tri
    tops = [jnp.max(x, axis=0, keepdims=True) for x in parts]
    top = tops[-1]
    for i in range(nk - 1):
        top = jnp.maximum(top, tops[i] - subs[i])
    top = top * SCALE_LOG2E
    weights = []
    for i in range(nk):
        low = top if i == nk - 1 else top + subs[i]
        weights.append(jnp.exp2(parts[i] * SCALE_LOG2E - low))
    total = sum(jnp.sum(x, axis=0, keepdims=True) for x in weights)
    inverse = 1.0 / total
    probs = jnp.concatenate([x * inverse for x in weights], axis=0)
    probs_b = probs.astype(BF16)
    weighted = probs * dprobs
    delta = jnp.sum(weighted, axis=0, keepdims=True)
    dscores = (weighted - probs * delta).astype(BF16)
    acc[1, slot, krows, :] += dot(probs_b, d2)
    acc[0, slot, krows, :] += dot(dscores, q2)
    dqt = dot(kw.T, dscores) * SCALE
    for h in range(HEADS):
        dq_v[slot, rows, h * HD : (h + 1) * HD] = dqt[:, h * HD : (h + 1) * HD].T.astype(BF16)


def kernel(
    n_ctx,
    n_head,
    q_hbm,
    do_hbm,
    k_hbm,
    v_hbm,
    doc_hbm,
    dq_hbm,
    dkv_hbm,
    q_v,
    do_v,
    dq_v,
    kv,
    acc,
    out_v,
    tail_out,
    tail_in,
    docs,
    load_sem,
    doc_sem,
    store_sem,
    kv_send,
    kv_recv,
    relay_send,
    relay_recv,
    tail_send,
    tail_recv,
    out_send,
    out_recv,
):
    c = lax.axis_index("ctx")
    x = lax.axis_index("head")
    after = lax.rem(c + 1, n_ctx)
    before = lax.rem(c + n_ctx - 1, n_ctx)
    is_first = c == 0
    is_last = c == n_ctx - 1
    first = jnp.where(is_first, 1, 0)

    barrier = pltpu.get_barrier_semaphore()
    for d in range(1, n_head):
        pl.semaphore_signal(
            barrier, inc=1, device_id=(c, lax.rem(x + d, n_head)), device_id_type=MESH
        )
    for other in (after, before):
        pl.semaphore_signal(barrier, inc=1, device_id=(other, x), device_id_type=MESH)

    doc_copy = pltpu.make_async_copy(doc_hbm, docs, doc_sem)
    doc_copy.start()
    sources = (k_hbm, v_hbm)

    def kv_place(which, slot, block):
        return kv.at[which, slot, pl.ds(at_block(block + 2), BLK), :]

    own = []
    for slot in range(2):
        for which in range(2):
            own.append(
                pltpu.make_async_copy(
                    sources[which].at[slot, :, pl.ds(at_block(x), HD)],
                    kv_place(which, slot, x),
                    kv_recv.at[which, slot, x],
                )
            )
            own[-1].start()
    loads = []
    for slot in range(2):
        for i, (src, dst) in enumerate(((q_hbm, q_v), (do_hbm, do_v))):
            loads.append(
                pltpu.make_async_copy(src.at[slot], dst.at[slot], load_sem.at[i, slot])
            )
            loads[-1].start()
    acc[...] = jnp.zeros_like(acc)
    kk = lax.broadcasted_iota(jnp.int32, (BLK, HEADS * BLK), 0)
    qq = lax.broadcasted_iota(jnp.int32, (BLK, HEADS * BLK), 1) % BLK
    tri = jnp.where(kk <= qq, 0.0, -BIG).astype(F32)

    pl.semaphore_wait(barrier, n_head + 1)

    sends = []
    for slot in range(2):
        for which in range(2):
            for d in (2, 1, 3):
                to = lax.rem(x + d, n_head)
                copy = pltpu.make_async_remote_copy(
                    src_ref=sources[which].at[slot, :, pl.ds(at_block(to), HD)],
                    dst_ref=kv_place(which, slot, x),
                    send_sem=kv_send.at[which, slot, d],
                    recv_sem=kv_recv.at[which, slot, x],
                    device_id=(c, to),
                    device_id_type=MESH,
                )
                copy.start()
                sends.append(copy)

    def wait_block(slot, block):
        for which in range(2):
            place = kv_place(which, slot, block)
            pltpu.make_async_copy(place, place, kv_recv.at[which, slot, block]).wait()

    def relay(slot):
        return pltpu.make_async_remote_copy(
            src_ref=kv.at[:, slot, pl.ds(SPAN, TAIL), :],
            dst_ref=kv.at[:, slot, pl.ds(0, TAIL), :],
            send_sem=relay_send.at[slot],
            recv_sem=relay_recv.at[slot],
            device_id=(after if slot == 0 else before, x),
            device_id_type=MESH,
        )

    def send_tail(slot):
        tail_out[slot, 0] = (acc[0, slot, 0:TAIL, :] * SCALE).astype(BF16)
        tail_out[slot, 1] = acc[1, slot, 0:TAIL, :].astype(BF16)
        copy = pltpu.make_async_remote_copy(
            src_ref=tail_out.at[slot],
            dst_ref=tail_in.at[slot],
            send_sem=tail_send.at[slot],
            recv_sem=tail_recv.at[slot],
            device_id=(before if slot == 0 else after, x),
            device_id_type=MESH,
        )
        copy.start()
        return copy

    def out_copies(slot, block):
        place = dkv_hbm.at[:, slot, :, pl.ds(at_block(x), HD)]
        remote = pltpu.make_async_remote_copy(
            src_ref=out_v.at[slot, block],
            dst_ref=place,
            send_sem=out_send.at[slot, block],
            recv_sem=out_recv.at[slot, x],
            device_id=(c, block),
            device_id_type=MESH,
        )
        local = pltpu.make_async_copy(out_v.at[slot, block], place, out_recv.at[slot, x])
        return remote, local

    def send_out(slot, block, extra=None):
        rows = pl.ds((block + 2) * BLK, BLK)
        for which in range(2):
            value = acc[which, slot, rows, :]
            if which == 0:
                value = value * SCALE
            if extra is not None:
                value = value + extra(which, block - 2)
            out_v[slot, block, which] = value.astype(BF16)
        remote, local = out_copies(slot, block)

        @pl.when(x != block)
        def _():
            remote.start()

        @pl.when(x == block)
        def _():
            local.start()

    spans = (c, 2 * n_ctx - 1 - c)
    tools = (q_v, do_v, dq_v, kv, acc, docs, tri)

    wait_block(0, 2)
    wait_block(0, 3)
    relays = [relay(0), relay(1)]
    relays[0].start()
    wait_block(0, 0)
    wait_block(0, 1)
    doc_copy.wait()
    loads[0].wait()
    loads[1].wait()
    block_grads(*tools, 0, spans[0], 3, 4, 2)
    block_grads(*tools, 0, spans[0], 2 - first, 3 - first, 2)
    for block in (2, 3, 0, 1):
        wait_block(1, block)
    relays[1].start()
    relays[0].wait_recv()
    block_grads(*tools, 0, spans[0], 0, 0, 3)
    block_grads(*tools, 0, spans[0], 1 + first, 1 + first, 3)
    tails = [send_tail(0)]
    send_out(0, 0)
    send_out(0, 1)
    stores = [pltpu.make_async_copy(dq_v.at[0], dq_hbm.at[0], store_sem.at[0])]
    stores[0].start()

    loads[2].wait()
    loads[3].wait()
    relays[1].wait_recv()

    @pl.when(is_last)
    def _():
        kv[:, 1, 0:TAIL, :] = kv[:, 0, SPAN : SPAN + TAIL, :]

    def store_rows(block):
        rows = pl.ds(block * BLK, BLK)
        stores.append(
            pltpu.make_async_copy(
                dq_v.at[1, rows, :], dq_hbm.at[1, rows, :], store_sem.at[1 + block]
            )
        )
        stores[-1].start()

    block_grads(*tools, 1, spans[1], 0, 0, 3)
    store_rows(0)
    block_grads(*tools, 1, spans[1], 1, 1, 3)
    store_rows(1)
    tails.append(send_tail(1))
    send_out(1, 0)
    block_grads(*tools, 1, spans[1], 2, 3, 2)
    store_rows(2)
    send_out(1, 1)
    tails[0].wait_recv()

    def extra_first(which, i):
        arrived = tail_in[0, which, i * BLK : (i + 1) * BLK, :].astype(F32)
        mine = tail_out[1, which, i * BLK : (i + 1) * BLK, :].astype(F32)
        return jnp.where(is_last, mine, arrived)

    def extra_second(which, i):
        arrived = tail_in[1, which, i * BLK : (i + 1) * BLK, :].astype(F32)
        return jnp.where(is_first, 0.0, arrived)

    send_out(0, 2, extra_first)
    send_out(0, 3, extra_first)
    block_grads(*tools, 1, spans[1], 3, 3, 3)
    store_rows(3)
    tails[1].wait_recv()
    send_out(1, 2, extra_second)
    send_out(1, 3, extra_second)

    for copy in sends + relays + tails:
        copy.wait_send()
    for slot in range(2):
        for block in range(4):
            remote, _ = out_copies(slot, block)

            @pl.when(x != block)
            def _():
                remote.wait_send()

            place = dkv_hbm.at[:, slot, :, pl.ds(block * HD, HD)]
            pltpu.make_async_copy(place, place, out_recv.at[slot, block]).wait()
    for copy in stores:
        copy.wait()


def per_device(n_ctx, n_head, query, key, value, d_out, doc_start):
    anywhere = pl.BlockSpec(memory_space=pl.ANY)
    dma = pltpu.SemaphoreType.DMA
    dq, dkv = pl.pallas_call(
        functools.partial(kernel, n_ctx, n_head),
        out_shape=(
            jax.ShapeDtypeStruct((2, SPAN, HEADS * HD), BF16),
            jax.ShapeDtypeStruct((2, 2, BLK, n_head * HD), BF16),
        ),
        in_specs=[anywhere] * 5,
        out_specs=(anywhere, anywhere),
        scratch_shapes=[
            pltpu.VMEM((2, SPAN, HEADS * HD), BF16),
            pltpu.VMEM((2, SPAN, HEADS * HD), BF16),
            pltpu.VMEM((2, SPAN, HEADS * HD), BF16),
            pltpu.VMEM((2, 2, EXT, HD), BF16),
            pltpu.VMEM((2, 2, EXT, HD), F32),
            pltpu.VMEM((2, 4, 2, BLK, HD), BF16),
            pltpu.VMEM((2, 2, TAIL, HD), BF16),
            pltpu.VMEM((2, 2, TAIL, HD), BF16),
            pltpu.SMEM(doc_start.shape, jnp.int32),
            dma((2, 2)),
            dma,
            dma((5,)),
            dma((2, 2, 4)),
            dma((2, 2, 4)),
            dma((2,)),
            dma((2,)),
            dma((2,)),
            dma((2,)),
            dma((2, 4)),
            dma((2, 4)),
        ],
        compiler_params=pltpu.CompilerParams(
            collective_id=0, has_side_effects=True, vmem_limit_bytes=56 << 20
        ),
    )(query[0], d_out[0], key[0], value[0], doc_start)
    return dq[None], dkv[0][None], dkv[1][None]


def solution(mesh):
    return jax.shard_map(
        functools.partial(per_device, mesh.shape["ctx"], mesh.shape["head"]),
        mesh=mesh,
        in_specs=(
            P("ctx", None, None, "head"),
            P("ctx", None, "head", None),
            P("ctx", None, "head", None),
            P("ctx", None, None, "head"),
            P(),
        ),
        out_specs=(
            P("ctx", None, None, "head"),
            P("ctx", None, "head", None),
            P("ctx", None, "head", None),
        ),
        check_vma=False,
    )
```

time: 144 us -> 39.1 us (0.27)
  the two profiles are of different devices: /device:TPU:22 before, /device:TPU:6 now
where the time goes in v1:
time: 39.1 us; the launch traced here: 39 us
  Pallas kernels  33.4 us (85%)
  local copies, waits for them, and re-layouts  4.93 us (13%)
  between operations  0.64 us (2%)
    pallas_call x1, Pallas kernels, per_device(): pl.pallas_call(functools.partial(kernel, n_ctx, n_head), out_shape=(jax.S...  33.4 us
    unnamed x1, local copies, waits for them, and re-layouts  3.08 us
    slice x1, local copies, waits for them, and re-layouts, per_device(): return (dq[None], dkv[0][None], dkv[1][None])  1.85 us

profile of v1, /device:TPU:6, one launch (start us, length us, event | category | flops | bytes accessed | tf_op | source)
XLA Modules:
  0.0 39.0 jit_solution(2023225933284006744)
XLA Ops:
  0.6 33.4 %shard_map.76 = (bf16[2,512,1024]{2,1,0:T(8,128)(2,1)}, bf16[2,2,128,512]{3,2,1,0:T(8,128)(2,1)}) custom-call(bf16[2,512,1024]{2,1,0:T(8,128)(2,1)} %bitcast.5, bf16[2,512,1024]{2,1,0:T(8,128)(2,1)} %bitcast.6, bf16[2,128,512]{2,1,0:T(8,128)(2,1)} %bitcast.8, bf16[2,128,512]{2,1,0:T(8,128)(2,1)} %bitcast.9, s32[512]{0:T(512)} %doc_hbm.1), custom_call_target="tpu_custom_call" | custom-call | tf_op jit(solution)/shard_map/pallas_call | solution.py:325
  34.1 1.9 %fusion = (bf16[1,2,128,512]{3,2,1,0:T(8,128)(2,1)}, bf16[1,2,128,512]{3,2,1,0:T(8,128)(2,1)}) fusion(bf16[2,2,128,512]{3,2,1,0:T(8,128)(2,1)} %get-tuple-element.6), kind=kLoop, calls=%fused_computation | loop fusion | bytes 1048576 | tf_op jit(solution)/shard_map/slice | solution.py:359
  35.9 3.1 %copy.9 = bf16[1,2,512,1024]{3,2,1,0:T(8,128)(2,1)} copy(bf16[1,2,512,1024]{3,2,1,0:T(8,128)(2,1)} %bitcast.7) | data formatting | bytes 4194304

commit v2 on v1

v2 whole, which is shorter than its diff:
```python
import functools

import jax
import jax.numpy as jnp
from jax import lax
from jax.experimental import pallas as pl
from jax.experimental.pallas import tpu as pltpu
from jax.sharding import PartitionSpec as P

F32 = jnp.float32
BF16 = jnp.bfloat16
HD = 128
BLK = 128
HEADS = 8
SPAN = 512
TAIL = 256
ROW = 16
EXT = TAIL + SPAN
SCALE = HD**-0.5
SCALE_LOG2E = SCALE * 1.4426950408889634
BIG = 1e30
NT = (((1,), (1,)), ((), ()))
NN = (((1,), (0,)), ((), ()))
MESH = pl.DeviceIdType.MESH


def dot(a, b, dims=NN):
    return lax.dot_general(a, b, dims, preferred_element_type=F32)


def at_block(index):
    if isinstance(index, int):
        return index * BLK
    return pl.multiple_of(index * BLK, BLK)


def block_grads(q_v, do_v, dq_v, kv, acc, docs, tri, slot, span, qb, k0, nk):
    rows = pl.ds(at_block(qb), BLK)
    krows = pl.ds(at_block(k0), nk * BLK)
    kw = kv[0, slot, krows, :]
    vw = kv[1, slot, krows, :]
    g = span * 4 + qb
    hidden = docs[g]
    hide = [hidden]
    for back in range(1, nk - 1):
        hidden = hidden + docs[jnp.maximum(g - back, 0)]
        hide.append(hidden)
    subs = [jnp.where(x > 0, BIG, 0.0).astype(F32) for x in hide][::-1]
    qq = q_v[slot, rows, :]
    dd = do_v[slot, rows, :]
    q2 = jnp.concatenate([qq[:, h * HD : (h + 1) * HD] for h in range(HEADS)], axis=0)
    d2 = jnp.concatenate([dd[:, h * HD : (h + 1) * HD] for h in range(HEADS)], axis=0)
    scores = dot(kw, q2, NT)
    dprobs = dot(vw, d2, NT)
    parts = [scores[i * BLK : (i + 1) * BLK] for i in range(nk)]
    parts[-1] = parts[-1] + tri
    tops = [jnp.max(x, axis=0, keepdims=True) for x in parts]
    top = tops[-1]
    for i in range(nk - 1):
        top = jnp.maximum(top, tops[i] - subs[i])
    top = top * SCALE_LOG2E
    weights = []
    for i in range(nk):
        low = top if i == nk - 1 else top + subs[i]
        weights.append(jnp.exp2(parts[i] * SCALE_LOG2E - low))
    total = sum(jnp.sum(x, axis=0, keepdims=True) for x in weights)
    inverse = 1.0 / total
    probs = jnp.concatenate([x * inverse for x in weights], axis=0)
    probs_b = probs.astype(BF16)
    weighted = probs * dprobs
    delta = jnp.sum(weighted, axis=0, keepdims=True)
    dscores = (weighted - probs * delta).astype(BF16)
    acc[1, slot, krows, :] += dot(probs_b, d2)
    acc[0, slot, krows, :] += dot(dscores, q2)
    dqt = dot(kw.T, dscores) * SCALE
    for h in range(HEADS):
        dq_v[slot, rows, h * HD : (h + 1) * HD] = dqt[:, h * HD : (h + 1) * HD].T.astype(BF16)


def kernel(
    n_ctx,
    n_head,
    q_hbm,
    do_hbm,
    k_hbm,
    v_hbm,
    doc_hbm,
    dq_v,
    dkv_v,
    stage,
    q_v,
    do_v,
    kv,
    acc,
    out_v,
    tail_out,
    tail_in,
    docs,
    stage_sem,
    load_sem,
    doc_sem,
    kv_send,
    kv_recv,
    relay_send,
    relay_recv,
    tail_send,
    tail_recv,
    out_send,
    out_recv,
    ready,
):
    c = lax.axis_index("ctx")
    x = lax.axis_index("head")
    is_first = c == 0
    is_last = c == n_ctx - 1
    first = jnp.where(is_first, 1, 0)
    row_start = lax.rem(c, ROW) == 0
    row_end = lax.rem(c, ROW) == ROW - 1
    early = jnp.logical_and(row_start, c > 0)
    late = jnp.logical_and(row_end, c < n_ctx - 1)
    lead = jnp.where(jnp.logical_or(early, late), 1, 0)

    barrier = pltpu.get_barrier_semaphore()

    def to_ctx(step):
        return (c + step, x)

    for d in range(1, n_head):
        pl.semaphore_signal(
            barrier, inc=1, device_id=(c, lax.rem(x + d, n_head)), device_id_type=MESH
        )

    @pl.when(c > 0)
    def _():
        pl.semaphore_signal(barrier, inc=1, device_id=to_ctx(-1), device_id_type=MESH)

    @pl.when(jnp.logical_not(row_end))
    def _():
        pl.semaphore_signal(barrier, inc=1, device_id=to_ctx(1), device_id_type=MESH)

    doc_copy = pltpu.make_async_copy(doc_hbm, docs, doc_sem)
    doc_copy.start()

    def kv_place(which, slot, block):
        return kv.at[which, slot, pl.ds(at_block(block + 2), BLK), :]

    staged = []
    for slot in range(2):
        for which, source in enumerate((k_hbm, v_hbm)):
            staged.append(
                pltpu.make_async_copy(
                    source.at[slot], stage.at[which, slot], stage_sem.at[which, slot]
                )
            )
            staged[-1].start()
            pltpu.make_async_copy(
                source.at[slot, :, pl.ds(at_block(x), HD)],
                kv_place(which, slot, x),
                kv_recv.at[which, slot, x],
            ).start()
    loads = []
    for slot in range(2):
        for i, (src, dst) in enumerate(((q_hbm, q_v), (do_hbm, do_v))):
            loads.append(
                pltpu.make_async_copy(src.at[slot], dst.at[slot], load_sem.at[i, slot])
            )
            loads[-1].start()
    acc[...] = jnp.zeros_like(acc)

    @pl.when(is_first)
    def _():
        kv[:, 0, 0:TAIL, :] = jnp.zeros((2, TAIL, HD), BF16)

    kk = lax.broadcasted_iota(jnp.int32, (BLK, HEADS * BLK), 0)
    qq = lax.broadcasted_iota(jnp.int32, (BLK, HEADS * BLK), 1) % BLK
    tri = jnp.where(kk <= qq, 0.0, -BIG).astype(F32)
    for copy in staged:
        copy.wait()

    partners = n_head - 1 + jnp.where(is_last, 0, 1) + jnp.where(row_start, 0, 1)
    pl.semaphore_wait(barrier, partners)

    @pl.when(late)
    def _():
        pl.semaphore_signal(ready, inc=1, device_id=to_ctx(1), device_id_type=MESH)

    sends = []
    for slot in range(2):
        for which in range(2):
            for d in (2, 1, 3):
                to = lax.rem(x + d, n_head)
                copy = pltpu.make_async_remote_copy(
                    src_ref=stage.at[which, slot, :, pl.ds(at_block(to), HD)],
                    dst_ref=kv_place(which, slot, x),
                    send_sem=kv_send.at[which, slot, d],
                    recv_sem=kv_recv.at[which, slot, x],
                    device_id=(c, to),
                    device_id_type=MESH,
                )
                copy.start()
                sends.append(copy)

    def wait_block(slot, block):
        for which in range(2):
            place = kv_place(which, slot, block)
            pltpu.make_async_copy(place, place, kv_recv.at[which, slot, block]).wait()

    def relay(slot, which, step):
        return pltpu.make_async_remote_copy(
            src_ref=kv.at[which, slot, pl.ds(SPAN, TAIL), :],
            dst_ref=kv.at[which, slot, pl.ds(0, TAIL), :],
            send_sem=relay_send.at[slot, which],
            recv_sem=relay_recv.at[slot, which],
            device_id=to_ctx(step),
            device_id_type=MESH,
        )

    def tail_copy(slot, step):
        return pltpu.make_async_remote_copy(
            src_ref=tail_out.at[slot],
            dst_ref=tail_in.at[slot],
            send_sem=tail_send.at[slot],
            recv_sem=tail_recv.at[slot],
            device_id=to_ctx(step),
            device_id_type=MESH,
        )

    def has(slot):
        if isinstance(slot, int):
            return jnp.logical_not(is_first) if slot == 0 else jnp.logical_not(is_last)
        return jnp.where(slot == 0, c > 0, c < n_ctx - 1)

    def send_tail(slot):
        tail_out[slot, 0] = (acc[0, slot, 0:TAIL, :] * SCALE).astype(BF16)
        tail_out[slot, 1] = acc[1, slot, 0:TAIL, :].astype(BF16)

        @pl.when(has(slot))
        def _():
            tail_copy(slot, 2 * slot - 1).start()

    def out_remote(slot, block):
        return pltpu.make_async_remote_copy(
            src_ref=out_v.at[slot, block],
            dst_ref=dkv_v.at[:, slot, :, pl.ds(at_block(x), HD)],
            send_sem=out_send.at[slot, block],
            recv_sem=out_recv.at[slot, x],
            device_id=(c, block),
            device_id_type=MESH,
        )

    def send_out(slot, block, extra=None):
        rows = pl.ds((block + 2) * BLK, BLK)
        for which in range(2):
            value = acc[which, slot, rows, :]
            if which == 0:
                value = value * SCALE
            if extra is not None:
                value = value + extra(which, block - 2)
            out_v[slot, block, which] = value.astype(BF16)

        @pl.when(x != block)
        def _():
            out_remote(slot, block).start()

        @pl.when(x == block)
        def _():
            place = dkv_v.at[:, slot, :, pl.ds(at_block(x), HD)]
            pltpu.make_async_copy(out_v.at[slot, block], place, out_recv.at[slot, x]).start()

    def span_of(slot):
        return jnp.where(slot == 0, c, 2 * n_ctx - 1 - c)

    tools = (q_v, do_v, dq_v, kv, acc, docs, tri)

    wait_block(0, 2)
    wait_block(0, 3)

    @pl.when(jnp.logical_not(is_last))
    def _():
        relay(0, 0, 1).start()
        relay(0, 1, 1).start()

    wait_block(0, 0)
    wait_block(0, 1)
    doc_copy.wait()
    loads[0].wait()
    loads[1].wait()
    block_grads(*tools, 0, span_of(0), 3, 4, 2)
    block_grads(*tools, 0, span_of(0), 2 - first, 3 - first, 2)
    for block in (2, 3, 0, 1):
        wait_block(1, block)

    @pl.when(early)
    def _():
        pl.semaphore_wait(ready, 1)

    @pl.when(jnp.logical_not(is_first))
    def _():
        relay(1, 0, -1).start()
        relay(1, 1, -1).start()

    @pl.when(is_last)
    def _():
        kv[:, 1, 0:TAIL, :] = kv[:, 0, SPAN : SPAN + TAIL, :]

    loads[2].wait()
    loads[3].wait()

    def front(slot):
        @pl.when(has(slot))
        def _():
            relay(slot, 0, 1).wait_recv()
            relay(slot, 1, 1).wait_recv()

        swap = jnp.where(slot == 0, first, 0)
        block_grads(*tools, slot, span_of(slot), 0, 0, 3)
        block_grads(*tools, slot, span_of(slot), 1 + swap, 1 + swap, 3)
        send_tail(slot)

    front(lead)
    front(1 - lead)
    send_out(0, 0)
    send_out(0, 1)
    send_out(1, 0)
    block_grads(*tools, 1, span_of(1), 3, 3, 3)

    def tail_arrives(slot):
        @pl.when(has(1 - slot))
        def _():
            tail_copy(slot, 1).wait_recv()

    def extra_first(which, i):
        arrived = tail_in[0, which, i * BLK : (i + 1) * BLK, :].astype(F32)
        mine = tail_out[1, which, i * BLK : (i + 1) * BLK, :].astype(F32)
        return jnp.where(is_last, mine, arrived)

    def extra_second(which, i):
        arrived = tail_in[1, which, i * BLK : (i + 1) * BLK, :].astype(F32)
        return jnp.where(is_first, 0.0, arrived)

    tail_arrives(0)
    send_out(0, 2, extra_first)
    send_out(0, 3, extra_first)
    block_grads(*tools, 1, span_of(1), 2, 3, 2)
    send_out(1, 1)
    tail_arrives(1)
    send_out(1, 2, extra_second)
    send_out(1, 3, extra_second)

    for copy in sends:
        copy.wait_send()
    for slot in range(2):

        @pl.when(has(1 - slot))
        def _():
            relay(slot, 0, 1).wait_send()
            relay(slot, 1, 1).wait_send()

        @pl.when(has(slot))
        def _():
            tail_copy(slot, 1).wait_send()

        for block in range(4):

            @pl.when(x != block)
            def _():
                out_remote(slot, block).wait_send()

            place = dkv_v.at[:, slot, :, pl.ds(block * HD, HD)]
            pltpu.make_async_copy(place, place, out_recv.at[slot, block]).wait()


def store_kernel(dq_v, dkv_v, dq_hbm, dk_hbm, dv_hbm, sem):
    copies = []
    for slot in range(2):
        for block in range(4):
            rows = pl.ds(block * BLK, BLK)
            copies.append((dq_v.at[slot, rows, :], dq_hbm.at[slot, rows, :]))
    copies.append((dkv_v.at[0], dk_hbm))
    copies.append((dkv_v.at[1], dv_hbm))
    started = [
        pltpu.make_async_copy(src, dst, sem.at[i]) for i, (src, dst) in enumerate(copies)
    ]
    for copy in started:
        copy.start()
    for copy in started:
        copy.wait()


def per_device(n_ctx, n_head, query, key, value, d_out, doc_start):
    hbm = pl.BlockSpec(memory_space=pltpu.HBM)
    vmem = pl.BlockSpec(memory_space=pltpu.VMEM)
    dma = pltpu.SemaphoreType.DMA
    dq, dkv = pl.pallas_call(
        functools.partial(kernel, n_ctx, n_head),
        out_shape=(
            jax.ShapeDtypeStruct((2, SPAN, HEADS * HD), BF16),
            jax.ShapeDtypeStruct((2, 2, BLK, n_head * HD), BF16),
        ),
        in_specs=[hbm] * 5,
        out_specs=(vmem, vmem),
        scratch_shapes=[
            pltpu.VMEM((2, 2, BLK, n_head * HD), BF16),
            pltpu.VMEM((2, SPAN, HEADS * HD), BF16),
            pltpu.VMEM((2, SPAN, HEADS * HD), BF16),
            pltpu.VMEM((2, 2, EXT, HD), BF16),
            pltpu.VMEM((2, 2, EXT, HD), F32),
            pltpu.VMEM((2, 4, 2, BLK, HD), BF16),
            pltpu.VMEM((2, 2, TAIL, HD), BF16),
            pltpu.VMEM((2, 2, TAIL, HD), BF16),
            pltpu.SMEM(doc_start.shape, jnp.int32),
            dma((2, 2)),
            dma((2, 2)),
            dma,
            dma((2, 2, 4)),
            dma((2, 2, 4)),
            dma((2, 2)),
            dma((2, 2)),
            dma((2,)),
            dma((2,)),
            dma((2, 4)),
            dma((2, 4)),
            pltpu.SemaphoreType.REGULAR,
        ],
        compiler_params=pltpu.CompilerParams(
            collective_id=0, has_side_effects=True, vmem_limit_bytes=40 << 20
        ),
    )(*[pltpu.with_memory_space_constraint(a, pltpu.HBM) for a in (query[0], d_out[0], key[0], value[0], doc_start)])
    d_query, d_key, d_value = pl.pallas_call(
        store_kernel,
        out_shape=(
            jax.ShapeDtypeStruct((2, SPAN, HEADS * HD), BF16),
            jax.ShapeDtypeStruct((2, BLK, n_head * HD), BF16),
            jax.ShapeDtypeStruct((2, BLK, n_head * HD), BF16),
        ),
        in_specs=[vmem, vmem],
        out_specs=(hbm, hbm, hbm),
        scratch_shapes=[dma((10,))],
        compiler_params=pltpu.CompilerParams(vmem_limit_bytes=1 << 20),
    )(dq, dkv)
    return d_query[None], d_key[None], d_value[None]


def solution(mesh):
    return jax.shard_map(
        functools.partial(per_device, mesh.shape["ctx"], mesh.shape["head"]),
        mesh=mesh,
        in_specs=(
            P("ctx", None, None, "head"),
            P("ctx", None, "head", None),
            P("ctx", None, "head", None),
            P("ctx", None, None, "head"),
            P(),
        ),
        out_specs=(
            P("ctx", None, None, "head"),
            P("ctx", None, "head", None),
            P("ctx", None, "head", None),
        ),
        check_vma=False,
    )
```

time: 39.1 us -> 30.9 us (0.79)
  the two profiles are of different devices: /device:TPU:6 before, /device:TPU:22 now
where the time goes in v2:
time: 30.9 us; the launch traced here: 30.8 us
  Pallas kernels  30.2 us (98%)
  between operations  0.64 us (2%)
    pallas_call x1, Pallas kernels, per_device(): pl.pallas_call(functools.partial(kernel, n_ctx, n_head), out_shape=(jax.S...  28.6 us
    pallas_call x1, Pallas kernels, per_device(): pl.pallas_call(store_kernel, out_shape=(jax.ShapeDtypeStruct((2, SPAN, HE...  1.57 us

profile of v2, /device:TPU:22, one launch (start us, length us, event | category | flops | bytes accessed | tf_op | source)
XLA Modules:
  0.0 30.8 jit_solution(18398590339985624890)
XLA Ops:
  0.6 28.6 %shard_map.76 = (bf16[2,512,1024]{2,1,0:T(8,128)(2,1)S(1)}, bf16[2,2,128,512]{3,2,1,0:T(8,128)(2,1)S(1)}) custom-call(bf16[2,512,1024]{2,1,0:T(8,128)(2,1)} %bitcast.7, bf16[2,512,1024]{2,1,0:T(8,128)(2,1)} %bitcast.8, bf16[2,128,512]{2,1,0:T(8,128)(2,1)} %bitcast.9, bf16[2,128,512]{2,1,0:T(8,128)(2,1)} %bitcast.10, s32[512]{0:T(512)} %doc_hbm.1), custom_call_target="tpu_custom_call" | custom-call | tf_op jit(solution)/shard_map/pallas_call | solution.py:394
  29.2 1.6 %shard_map.77 = (bf16[2,512,1024]{2,1,0:T(8,128)(2,1)}, bf16[2,128,512]{2,1,0:T(8,128)(2,1)}, bf16[2,128,512]{2,1,0:T(8,128)(2,1)}) custom-call(bf16[2,512,1024]{2,1,0:T(8,128)(2,1)S(1)} %get-tuple-element.8.dq_v, bf16[2,2,128,512]{3,2,1,0:T(8,128)(2,1)S(1)} %get-tuple-element.9.dkv_v), custom_call_target="tpu_custom_call" | custom-call | tf_op jit(solution)/shard_map/pallas_call | solution.py:429

commit v3 on v2

--- a/solution.py
+++ b/solution.py
@@ -65,11 +65,10 @@
         weights.append(jnp.exp2(parts[i] * SCALE_LOG2E - low))
     total = sum(jnp.sum(x, axis=0, keepdims=True) for x in weights)
     inverse = 1.0 / total
-    probs = jnp.concatenate([x * inverse for x in weights], axis=0)
-    probs_b = probs.astype(BF16)
-    weighted = probs * dprobs
-    delta = jnp.sum(weighted, axis=0, keepdims=True)
-    dscores = (weighted - probs * delta).astype(BF16)
+    weights = jnp.concatenate(weights, axis=0)
+    probs_b = (weights * inverse).astype(BF16)
+    delta = inverse * jnp.sum(weights * dprobs, axis=0, keepdims=True)
+    dscores = (weights * inverse * (dprobs - delta)).astype(BF16)
     acc[1, slot, krows, :] += dot(probs_b, d2)
     acc[0, slot, krows, :] += dot(dscores, q2)
     dqt = dot(kw.T, dscores) * SCALE
@@ -141,8 +140,8 @@
     doc_copy = pltpu.make_async_copy(doc_hbm, docs, doc_sem)
     doc_copy.start()
 
-    def kv_place(which, slot, block):
-        return kv.at[which, slot, pl.ds(at_block(block + 2), BLK), :]
+    def kv_place(slot, block):
+        return kv.at[:, slot, pl.ds(at_block(block + 2), BLK), :]
 
     staged = []
     for slot in range(2):
@@ -153,11 +152,6 @@
                 )
             )
             staged[-1].start()
-            pltpu.make_async_copy(
-                source.at[slot, :, pl.ds(at_block(x), HD)],
-                kv_place(which, slot, x),
-                kv_recv.at[which, slot, x],
-            ).start()
     loads = []
     for slot in range(2):
         for i, (src, dst) in enumerate(((q_hbm, q_v), (do_hbm, do_v))):
@@ -176,6 +170,10 @@
     tri = jnp.where(kk <= qq, 0.0, -BIG).astype(F32)
     for copy in staged:
         copy.wait()
+    for which in range(2):
+        for slot in range(2):
+            mine = stage[which, slot, :, pl.ds(at_block(x), HD)]
+            kv[which, slot, pl.ds(at_block(x + 2), BLK), :] = mine
 
     partners = n_head - 1 + jnp.where(is_last, 0, 1) + jnp.where(row_start, 0, 1)
     pl.semaphore_wait(barrier, partners)
@@ -186,41 +184,41 @@
 
     sends = []
     for slot in range(2):
-        for which in range(2):
-            for d in (2, 1, 3):
-                to = lax.rem(x + d, n_head)
-                copy = pltpu.make_async_remote_copy(
-                    src_ref=stage.at[which, slot, :, pl.ds(at_block(to), HD)],
-                    dst_ref=kv_place(which, slot, x),
-                    send_sem=kv_send.at[which, slot, d],
-                    recv_sem=kv_recv.at[which, slot, x],
-                    device_id=(c, to),
-                    device_id_type=MESH,
-                )
-                copy.start()
-                sends.append(copy)
-
-    def wait_block(slot, block):
-        for which in range(2):
-            place = kv_place(which, slot, block)
-            pltpu.make_async_copy(place, place, kv_recv.at[which, slot, block]).wait()
-
-    def relay(slot, which, step):
+        for d in (2, 1, 3):
+            to = lax.rem(x + d, n_head)
+            copy = pltpu.make_async_remote_copy(
+                src_ref=stage.at[:, slot, :, pl.ds(at_block(to), HD)],
+                dst_ref=kv_place(slot, x),
+                send_sem=kv_send.at[slot, d],
+                recv_sem=kv_recv.at[slot, x],
+                device_id=(c, to),
+                device_id_type=MESH,
+            )
+            copy.start()
+            sends.append(copy)
+
+    def wait_kv(slot, block):
+        @pl.when(x != block)
+        def _():
+            place = kv_place(slot, block)
+            pltpu.make_async_copy(place, place, kv_recv.at[slot, block]).wait()
+
+    def relay(slot, step):
         return pltpu.make_async_remote_copy(
-            src_ref=kv.at[which, slot, pl.ds(SPAN, TAIL), :],
-            dst_ref=kv.at[which, slot, pl.ds(0, TAIL), :],
-            send_sem=relay_send.at[slot, which],
-            recv_sem=relay_recv.at[slot, which],
+            src_ref=kv.at[:, slot, pl.ds(SPAN, TAIL), :],
+            dst_ref=kv.at[:, slot, pl.ds(0, TAIL), :],
+            send_sem=relay_send.at[slot],
+            recv_sem=relay_recv.at[slot],
             device_id=to_ctx(step),
             device_id_type=MESH,
         )
 
-    def tail_copy(slot, step):
+    def tail_copy(slot, i, step):
         return pltpu.make_async_remote_copy(
-            src_ref=tail_out.at[slot],
-            dst_ref=tail_in.at[slot],
-            send_sem=tail_send.at[slot],
-            recv_sem=tail_recv.at[slot],
+            src_ref=tail_out.at[slot, i],
+            dst_ref=tail_in.at[slot, i],
+            send_sem=tail_send.at[slot, i],
+            recv_sem=tail_recv.at[slot, i],
             device_id=to_ctx(step),
             device_id_type=MESH,
         )
@@ -230,13 +228,14 @@
             return jnp.logical_not(is_first) if slot == 0 else jnp.logical_not(is_last)
         return jnp.where(slot == 0, c > 0, c < n_ctx - 1)
 
-    def send_tail(slot):
-        tail_out[slot, 0] = (acc[0, slot, 0:TAIL, :] * SCALE).astype(BF16)
-        tail_out[slot, 1] = acc[1, slot, 0:TAIL, :].astype(BF16)
+    def send_tail(slot, i):
+        rows = pl.ds(i * BLK, BLK)
+        tail_out[slot, i, 0] = (acc[0, slot, rows, :] * SCALE).astype(BF16)
+        tail_out[slot, i, 1] = acc[1, slot, rows, :].astype(BF16)
 
         @pl.when(has(slot))
         def _():
-            tail_copy(slot, 2 * slot - 1).start()
+            tail_copy(slot, i, 2 * slot - 1).start()
 
     def out_remote(slot, block):
         return pltpu.make_async_remote_copy(
@@ -272,32 +271,34 @@
 
     tools = (q_v, do_v, dq_v, kv, acc, docs, tri)
 
-    wait_block(0, 2)
-    wait_block(0, 3)
+    wait_kv(0, 3)
+    wait_kv(0, 2)
 
     @pl.when(jnp.logical_not(is_last))
     def _():
-        relay(0, 0, 1).start()
-        relay(0, 1, 1).start()
-
-    wait_block(0, 0)
-    wait_block(0, 1)
+        relay(0, 1).start()
+
     doc_copy.wait()
     loads[0].wait()
     loads[1].wait()
+    wait_kv(0, 1)
+    wait_kv(0, 0)
     block_grads(*tools, 0, span_of(0), 3, 4, 2)
     block_grads(*tools, 0, span_of(0), 2 - first, 3 - first, 2)
-    for block in (2, 3, 0, 1):
-        wait_block(1, block)
 
     @pl.when(early)
     def _():
         pl.semaphore_wait(ready, 1)
 
+    wait_kv(1, 3)
+    wait_kv(1, 2)
+
     @pl.when(jnp.logical_not(is_first))
     def _():
-        relay(1, 0, -1).start()
-        relay(1, 1, -1).start()
+        relay(1, -1).start()
+
+    wait_kv(1, 1)
+    wait_kv(1, 0)
 
     @pl.when(is_last)
     def _():
@@ -309,43 +310,68 @@
     def front(slot):
         @pl.when(has(slot))
         def _():
-            relay(slot, 0, 1).wait_recv()
-            relay(slot, 1, 1).wait_recv()
+            relay(slot, 1).wait_recv()
 
         swap = jnp.where(slot == 0, first, 0)
         block_grads(*tools, slot, span_of(slot), 0, 0, 3)
         block_grads(*tools, slot, span_of(slot), 1 + swap, 1 + swap, 3)
-        send_tail(slot)
+        send_tail(slot, 0)
+        send_tail(slot, 1)
 
     front(lead)
+
+    @pl.when(lead == 0)
+    def _():
+        send_out(0, 0)
+        send_out(0, 1)
+
+    @pl.when(lead == 1)
+    def _():
+        send_out(1, 0)
+
     front(1 - lead)
-    send_out(0, 0)
-    send_out(0, 1)
-    send_out(1, 0)
-    block_grads(*tools, 1, span_of(1), 3, 3, 3)
-
-    def tail_arrives(slot):
+
+    @pl.when(lead == 1)
+    def _():
+        send_out(0, 0)
+        send_out(0, 1)
+
+    @pl.when(lead == 0)
+    def _():
+        send_out(1, 0)
+
+    def tail_arrives(slot, i):
         @pl.when(has(1 - slot))
         def _():
-            tail_copy(slot, 1).wait_recv()
+            tail_copy(slot, i, 1).wait_recv()
 
     def extra_first(which, i):
-        arrived = tail_in[0, which, i * BLK : (i + 1) * BLK, :].astype(F32)
-        mine = tail_out[1, which, i * BLK : (i + 1) * BLK, :].astype(F32)
+        arrived = tail_in[0, i, which].astype(F32)
+        mine = tail_out[1, i, which].astype(F32)
         return jnp.where(is_last, mine, arrived)
 
     def extra_second(which, i):
-        arrived = tail_in[1, which, i * BLK : (i + 1) * BLK, :].astype(F32)
-        return jnp.where(is_first, 0.0, arrived)
-
-    tail_arrives(0)
-    send_out(0, 2, extra_first)
-    send_out(0, 3, extra_first)
-    block_grads(*tools, 1, span_of(1), 2, 3, 2)
+        return jnp.where(is_first, 0.0, tail_in[1, i, which].astype(F32))
+
+    for i in range(2):
+        tail_arrives(0, i)
+        send_out(0, 2 + i, extra_first)
+
+    @pl.when(is_first)
+    def _():
+        block_grads(*tools, 1, span_of(1), 2, 3, 2)
+        block_grads(*tools, 1, span_of(1), 3, 3, 3)
+
+    @pl.when(jnp.logical_not(is_first))
+    def _():
+        block_grads(*tools, 1, span_of(1), 2, 3, 2)
+        block_grads(*tools, 1, span_of(1), 3, 4, 2)
+
     send_out(1, 1)
-    tail_arrives(1)
-    send_out(1, 2, extra_second)
-    send_out(1, 3, extra_second)
+
+    for i in range(2):
+        tail_arrives(1, i)
+        send_out(1, 2 + i, extra_second)
 
     for copy in sends:
         copy.wait_send()
@@ -353,12 +379,12 @@
 
         @pl.when(has(1 - slot))
         def _():
-            relay(slot, 0, 1).wait_send()
-            relay(slot, 1, 1).wait_send()
+            relay(slot, 1).wait_send()
 
         @pl.when(has(slot))
         def _():
-            tail_copy(slot, 1).wait_send()
+            tail_copy(slot, 0, 1).wait_send()
+            tail_copy(slot, 1, 1).wait_send()
 
         for block in range(4):
 
@@ -406,18 +432,18 @@
             pltpu.VMEM((2, 2, EXT, HD), BF16),
             pltpu.VMEM((2, 2, EXT, HD), F32),
             pltpu.VMEM((2, 4, 2, BLK, HD), BF16),
-            pltpu.VMEM((2, 2, TAIL, HD), BF16),
-            pltpu.VMEM((2, 2, TAIL, HD), BF16),
+            pltpu.VMEM((2, 2, 2, BLK, HD), BF16),
+            pltpu.VMEM((2, 2, 2, BLK, HD), BF16),
             pltpu.SMEM(doc_start.shape, jnp.int32),
             dma((2, 2)),
             dma((2, 2)),
             dma,
-            dma((2, 2, 4)),
-            dma((2, 2, 4)),
+            dma((2, 4)),
+            dma((2, 4)),
+            dma((2,)),
+            dma((2,)),
             dma((2, 2)),
             dma((2, 2)),
-            dma((2,)),
-            dma((2,)),
             dma((2, 4)),
             dma((2, 4)),
             pltpu.SemaphoreType.REGULAR,
@@ -425,7 +451,10 @@
         compiler_params=pltpu.CompilerParams(
             collective_id=0, has_side_effects=True, vmem_limit_bytes=40 << 20
         ),
-    )(*[pltpu.with_memory_space_constraint(a, pltpu.HBM) for a in (query[0], d_out[0], key[0], value[0], doc_start)])
+    )(*[
+            pltpu.with_memory_space_constraint(a, pltpu.HBM)
+            for a in (query[0], d_out[0], key[0], value[0], doc_start)
+        ])
     d_query, d_key, d_value = pl.pallas_call(
         store_kernel,
         out_shape=(

time: 30.9 us -> 30.3 us (0.981)
  Pallas kernels: 30.2 us -> 29.6 us
    pallas_call x1, Pallas kernels: 28.6 us -> 28 us  [per_device(): pl.pallas_call(functools.partial(kernel, n_ctx, n_head), out_shape=(jax.S...]
where the time goes in v3:
time: 30.3 us; the launch traced here: 30.2 us
  Pallas kernels  29.6 us (98%)
  between operations  0.64 us (2%)
    pallas_call x1, Pallas kernels, per_device(): pl.pallas_call(functools.partial(kernel, n_ctx, n_head), out_shape=(jax.S...  28 us
    pallas_call x1, Pallas kernels, per_device(): pl.pallas_call(store_kernel, out_shape=(jax.ShapeDtypeStruct((2, SPAN, HE...  1.57 us

profile of v3, /device:TPU:22, one launch (start us, length us, event | category | flops | bytes accessed | tf_op | source)
XLA Modules:
  0.0 30.2 jit_solution(5714821538486203845)
XLA Ops:
  0.6 28.0 %shard_map.76 = (bf16[2,512,1024]{2,1,0:T(8,128)(2,1)S(1)}, bf16[2,2,128,512]{3,2,1,0:T(8,128)(2,1)S(1)}) custom-call(bf16[2,512,1024]{2,1,0:T(8,128)(2,1)} %bitcast.7, bf16[2,512,1024]{2,1,0:T(8,128)(2,1)} %bitcast.8, bf16[2,128,512]{2,1,0:T(8,128)(2,1)} %bitcast.9, bf16[2,128,512]{2,1,0:T(8,128)(2,1)} %bitcast.10, s32[512]{0:T(512)} %doc_hbm.1), custom_call_target="tpu_custom_call" | custom-call | tf_op jit(solution)/shard_map/pallas_call | solution.py:420
  28.6 1.6 %shard_map.77 = (bf16[2,512,1024]{2,1,0:T(8,128)(2,1)}, bf16[2,128,512]{2,1,0:T(8,128)(2,1)}, bf16[2,128,512]{2,1,0:T(8,128)(2,1)}) custom-call(bf16[2,512,1024]{2,1,0:T(8,128)(2,1)S(1)} %get-tuple-element.8.dq_v, bf16[2,2,128,512]{3,2,1,0:T(8,128)(2,1)S(1)} %get-tuple-element.9.dkv_v), custom_call_target="tpu_custom_call" | custom-call | tf_op jit(solution)/shard_map/pallas_call | solution.py:458

commit v4 on v3

--- a/solution.py
+++ b/solution.py
@@ -152,29 +152,8 @@
                 )
             )
             staged[-1].start()
-    loads = []
-    for slot in range(2):
-        for i, (src, dst) in enumerate(((q_hbm, q_v), (do_hbm, do_v))):
-            loads.append(
-                pltpu.make_async_copy(src.at[slot], dst.at[slot], load_sem.at[i, slot])
-            )
-            loads[-1].start()
-    acc[...] = jnp.zeros_like(acc)
-
-    @pl.when(is_first)
-    def _():
-        kv[:, 0, 0:TAIL, :] = jnp.zeros((2, TAIL, HD), BF16)
-
-    kk = lax.broadcasted_iota(jnp.int32, (BLK, HEADS * BLK), 0)
-    qq = lax.broadcasted_iota(jnp.int32, (BLK, HEADS * BLK), 1) % BLK
-    tri = jnp.where(kk <= qq, 0.0, -BIG).astype(F32)
     for copy in staged:
         copy.wait()
-    for which in range(2):
-        for slot in range(2):
-            mine = stage[which, slot, :, pl.ds(at_block(x), HD)]
-            kv[which, slot, pl.ds(at_block(x + 2), BLK), :] = mine
-
     partners = n_head - 1 + jnp.where(is_last, 0, 1) + jnp.where(row_start, 0, 1)
     pl.semaphore_wait(barrier, partners)
 
@@ -196,6 +175,28 @@
             )
             copy.start()
             sends.append(copy)
+
+    loads = []
+    for slot in range(2):
+        for i, (src, dst) in enumerate(((q_hbm, q_v), (do_hbm, do_v))):
+            loads.append(
+                pltpu.make_async_copy(src.at[slot], dst.at[slot], load_sem.at[i, slot])
+            )
+            loads[-1].start()
+    for which in range(2):
+        for slot in range(2):
+            mine = stage[which, slot, :, pl.ds(at_block(x), HD)]
+            kv[which, slot, pl.ds(at_block(x + 2), BLK), :] = mine
+
+    acc[...] = jnp.zeros_like(acc)
+
+    @pl.when(is_first)
+    def _():
+        kv[:, 0, 0:TAIL, :] = jnp.zeros((2, TAIL, HD), BF16)
+
+    kk = lax.broadcasted_iota(jnp.int32, (BLK, HEADS * BLK), 0)
+    qq = lax.broadcasted_iota(jnp.int32, (BLK, HEADS * BLK), 1) % BLK
+    tri = jnp.where(kk <= qq, 0.0, -BIG).astype(F32)
 
     def wait_kv(slot, block):
         @pl.when(x != block)

time: 30.3 us -> 29.6 us (0.977)
  Pallas kernels: 29.6 us -> 28.9 us
    pallas_call x1, Pallas kernels: 28 us -> 27.3 us  [per_device(): pl.pallas_call(functools.partial(kernel, n_ctx, n_head), out_shape=(jax.S...]
where the time goes in v4:
time: 29.6 us; the launch traced here: 29.5 us
  Pallas kernels  28.9 us (98%)
  between operations  0.64 us (2%)
    pallas_call x1, Pallas kernels, per_device(): pl.pallas_call(functools.partial(kernel, n_ctx, n_head), out_shape=(jax.S...  27.3 us
    pallas_call x1, Pallas kernels, per_device(): pl.pallas_call(store_kernel, out_shape=(jax.ShapeDtypeStruct((2, SPAN, HE...  1.57 us

profile of v4, /device:TPU:22, one launch (start us, length us, event | category | flops | bytes accessed | tf_op | source)
XLA Modules:
  0.0 29.5 jit_solution(14613307385222684081)
XLA Ops:
  0.6 27.3 %shard_map.76 = (bf16[2,512,1024]{2,1,0:T(8,128)(2,1)S(1)}, bf16[2,2,128,512]{3,2,1,0:T(8,128)(2,1)S(1)}) custom-call(bf16[2,512,1024]{2,1,0:T(8,128)(2,1)} %bitcast.7, bf16[2,512,1024]{2,1,0:T(8,128)(2,1)} %bitcast.8, bf16[2,128,512]{2,1,0:T(8,128)(2,1)} %bitcast.9, bf16[2,128,512]{2,1,0:T(8,128)(2,1)} %bitcast.10, s32[512]{0:T(512)} %doc_hbm.1), custom_call_target="tpu_custom_call" | custom-call | tf_op jit(solution)/shard_map/pallas_call | solution.py:421
  27.9 1.6 %shard_map.77 = (bf16[2,512,1024]{2,1,0:T(8,128)(2,1)}, bf16[2,128,512]{2,1,0:T(8,128)(2,1)}, bf16[2,128,512]{2,1,0:T(8,128)(2,1)}) custom-call(bf16[2,512,1024]{2,1,0:T(8,128)(2,1)S(1)} %get-tuple-element.8.dq_v, bf16[2,2,128,512]{3,2,1,0:T(8,128)(2,1)S(1)} %get-tuple-element.9.dkv_v), custom_call_target="tpu_custom_call" | custom-call | tf_op jit(solution)/shard_map/pallas_call | solution.py:459

commit v5 on v4

--- a/solution.py
+++ b/solution.py
@@ -68,7 +68,7 @@
     weights = jnp.concatenate(weights, axis=0)
     probs_b = (weights * inverse).astype(BF16)
     delta = inverse * jnp.sum(weights * dprobs, axis=0, keepdims=True)
-    dscores = (weights * inverse * (dprobs - delta)).astype(BF16)
+    dscores = probs_b * (dprobs - delta).astype(BF16)
     acc[1, slot, krows, :] += dot(probs_b, d2)
     acc[0, slot, krows, :] += dot(dscores, q2)
     dqt = dot(kw.T, dscores) * SCALE

time: 29.6 us -> 29.4 us (level)
  no operation moved by 1% of the time
where the time goes in v5:
time: 29.4 us; the launch traced here: 29.3 us
  Pallas kernels  28.7 us (98%)
  between operations  0.64 us (2%)
    pallas_call x1, Pallas kernels, per_device(): pl.pallas_call(functools.partial(kernel, n_ctx, n_head), out_shape=(jax.S...  27.1 us
    pallas_call x1, Pallas kernels, per_device(): pl.pallas_call(store_kernel, out_shape=(jax.ShapeDtypeStruct((2, SPAN, HE...  1.57 us

profile of v5, /device:TPU:22, one launch (start us, length us, event | category | flops | bytes accessed | tf_op | source)
XLA Modules:
  0.0 29.3 jit_solution(1064593759856172061)
XLA Ops:
  0.6 27.1 %shard_map.76 = (bf16[2,512,1024]{2,1,0:T(8,128)(2,1)S(1)}, bf16[2,2,128,512]{3,2,1,0:T(8,128)(2,1)S(1)}) custom-call(bf16[2,512,1024]{2,1,0:T(8,128)(2,1)} %bitcast.7, bf16[2,512,1024]{2,1,0:T(8,128)(2,1)} %bitcast.8, bf16[2,128,512]{2,1,0:T(8,128)(2,1)} %bitcast.9, bf16[2,128,512]{2,1,0:T(8,128)(2,1)} %bitcast.10, s32[512]{0:T(512)} %doc_hbm.1), custom_call_target="tpu_custom_call" | custom-call | tf_op jit(solution)/shard_map/pallas_call | solution.py:421
  27.8 1.6 %shard_map.77 = (bf16[2,512,1024]{2,1,0:T(8,128)(2,1)}, bf16[2,128,512]{2,1,0:T(8,128)(2,1)}, bf16[2,128,512]{2,1,0:T(8,128)(2,1)}) custom-call(bf16[2,512,1024]{2,1,0:T(8,128)(2,1)S(1)} %get-tuple-element.8.dq_v, bf16[2,2,128,512]{3,2,1,0:T(8,128)(2,1)S(1)} %get-tuple-element.9.dkv_v), custom_call_target="tpu_custom_call" | custom-call | tf_op jit(solution)/shard_map/pallas_call | solution.py:459
